TPU v7x, 32 devices: a whole 2x2x4 slice. The times are simulated.
32 devices in a mesh: dp: 8 (over z, y), seq: 4 (over x, core).
Axes of the slice: x: 2, y: 2, z: 4, core: 2. Of those that a mesh axis runs over, the one named last changes fastest.
Arguments:
- tokens: bfloat16 [16, 2048, 768], P('dp', 'seq'), may hold values from -6 to 6
- cotangent: bfloat16 [16, 2048, 768], P('dp', 'seq'), may hold values from -6 to 6
- lengths: int32 [16], replicated, may hold values from 513 to 1984, as said below
- norm_gains: float32 [768, 2], P(('dp', 'seq')), may hold values from 0.1 to 1.9
- shift_taps: float32 [768, 64], P(('dp', 'seq')), may hold values from -0.75 to 0.75
- decay_rate: float32 [768, 32], P(('dp', 'seq')), may hold values from 0.0001 to 0.05
- frequency: float32 [768, 32], P(('dp', 'seq')), may hold values from 0 to 1
- mode_coef: float32 [768, 2, 32], P(('dp', 'seq')), may hold values from -0.036 to 0.036
- skip_gain: float32 [768], P(('dp', 'seq')), may hold values from -6 to 6
- qkv_weight: bfloat16 [768, 2304], P(('dp', 'seq')), may hold values from -0.21875 to 0.21875
- out_weight: bfloat16 [768, 768], P(('dp', 'seq')), may hold values from -0.21875 to 0.21875
- up_weight: bfloat16 [768, 3072], P(('dp', 'seq')), may hold values from -0.21875 to 0.21875
- down_weight: bfloat16 [3072, 768], P(('dp', 'seq')), may hold values from -0.109375 to 0.109375
Outputs:
- layer_out: bfloat16 [16, 2048, 768], P('dp', 'seq')
- input_grad: float32 [16, 2048, 768], P('dp', 'seq')
- norm_gains_grad: float32 [768, 2], P(('dp', 'seq'))
- shift_taps_grad: float32 [768, 64], P(('dp', 'seq'))
- decay_rate_grad: float32 [768, 32], P(('dp', 'seq'))
- frequency_grad: float32 [768, 32], P(('dp', 'seq'))
- mode_coef_grad: float32 [768, 2, 32], P(('dp', 'seq'))
- skip_gain_grad: float32 [768], P(('dp', 'seq'))
- qkv_weight_grad: float32 [768, 2304], P(('dp', 'seq'))
- out_weight_grad: float32 [768, 768], P(('dp', 'seq'))
- up_weight_grad: float32 [768, 3072], P(('dp', 'seq'))
- down_weight_grad: float32 [3072, 768], P(('dp', 'seq'))
Inputs may be any that keep to these rules, and one draw needn't show every extreme that they name: `lengths`: slots 2i and 2i + 1 together hold exactly 40 blocks of 64 positions that contain a live position, a partly live block counting as one.
All inputs are finite; a program needn't handle non-finite values.
Results may differ from a plain program's by a relative error of at most 0.011.
Values may be sent and summed in bfloat16 or wider, within the bound.
A program may use at most 192 MiB of HBM per device.

v0:
```python
import math

import jax
import jax.numpy as jnp
from jax import lax
from jax.sharding import PartitionSpec as P

SLOT = 2048
BLK = 64


highest = lax.Precision.HIGHEST


def layer_norm(row_block, gain):
    center = row_block - jnp.mean(row_block, axis=-1, keepdims=True)
    spread = jnp.mean(center * center, axis=-1, keepdims=True)
    return center * lax.rsqrt(spread + 1e-05) * gain


def exact_gelu(values):
    return jax.nn.gelu(values, approximate=False)


def mat_dot(left, right, contract):
    return lax.dot_general(left, right, (contract, ((), ())), preferred_element_type=jnp.float32)


def dft_tables(length):
    first_size = math.gcd(length, 128)
    second_size = length // first_size

    def dft_table(size):
        indices = jnp.arange(size, dtype=jnp.int32)
        angles = (indices[:, None] * indices[None, :] % size).astype(jnp.float32) * (
            2.0 * math.pi / size
        )
        return (jnp.cos(angles), jnp.sin(angles))

    cos_first, sin_first = dft_table(first_size)
    cos_second, sin_second = dft_table(second_size)
    outer_ids = jnp.arange(first_size, dtype=jnp.int32)[:, None]
    inner_ids = jnp.arange(second_size, dtype=jnp.int32)[None, :]
    twiddle = (outer_ids * inner_ids % length).astype(jnp.float32) * (2.0 * math.pi / length)
    return (
        first_size,
        second_size,
        cos_first,
        sin_first,
        cos_second,
        sin_second,
        jnp.cos(twiddle),
        jnp.sin(twiddle),
    )


def forward_dft(signal, tables):
    (
        first_size,
        second_size,
        cos_first,
        sin_first,
        cos_second,
        sin_second,
        twiddle_cos,
        twiddle_sin,
    ) = tables
    shaped = signal.reshape(signal.shape[:-1] + (first_size, second_size))
    real_one = jnp.einsum("kn,...nm->...km", cos_first, shaped, precision=highest)
    imag_one = -jnp.einsum("kn,...nm->...km", sin_first, shaped, precision=highest)
    real_two = real_one * twiddle_cos + imag_one * twiddle_sin
    imag_two = imag_one * twiddle_cos - real_one * twiddle_sin
    real_out = jnp.einsum("...kn,nm->...km", real_two, cos_second, precision=highest) + jnp.einsum(
        "...kn,nm->...km", imag_two, sin_second, precision=highest
    )
    imag_out = jnp.einsum("...kn,nm->...km", imag_two, cos_second, precision=highest) - jnp.einsum(
        "...kn,nm->...km", real_two, sin_second, precision=highest
    )
    return (real_out, imag_out)


def inverse_dft(real_in, imag_in, tables, keep_count):
    (
        first_size,
        second_size,
        cos_first,
        sin_first,
        cos_second,
        sin_second,
        twiddle_cos,
        twiddle_sin,
    ) = tables
    real_one = jnp.einsum("...kn,nm->...km", real_in, cos_second, precision=highest) - jnp.einsum(
        "...kn,nm->...km", imag_in, sin_second, precision=highest
    )
    imag_one = jnp.einsum("...kn,nm->...km", imag_in, cos_second, precision=highest) + jnp.einsum(
        "...kn,nm->...km", real_in, sin_second, precision=highest
    )
    real_two = real_one * twiddle_cos - imag_one * twiddle_sin
    imag_two = imag_one * twiddle_cos + real_one * twiddle_sin
    joined = jnp.einsum("nk,...km->...nm", cos_first, real_two, precision=highest) - jnp.einsum(
        "nk,...km->...nm", sin_first, imag_two, precision=highest
    )
    joined = joined / float(first_size * second_size)
    return joined.reshape(joined.shape[:-2] + (first_size * second_size,))[..., :keep_count]


def kernel_spectrum(kernel, total, tables):
    padded = jnp.pad(kernel, ((0, 0), (0, total - kernel.shape[-1])))
    real_out, imag_out = forward_dft(padded, tables)
    return (real_out[:, None], imag_out[:, None])


def causal_conv(signal, kernel_real, kernel_imag, tables):
    length = signal.shape[-1]
    padded = jnp.concatenate([signal, jnp.zeros_like(signal)], axis=-1)
    real_in, imag_in = forward_dft(padded, tables)
    return inverse_dft(
        real_in * kernel_real - imag_in * kernel_imag,
        real_in * kernel_imag + imag_in * kernel_real,
        tables,
        length,
    )


def mode_kernel(decay_part, freq_part, coef_part, length):
    positions = jnp.arange(length).astype(decay_part.dtype)
    fading = jnp.exp(-decay_part[:, :, None] * positions)
    turning = freq_part[:, :, None] * positions
    wave = coef_part[:, 0, :, None] * jnp.cos(turning) - coef_part[:, 1, :, None] * jnp.sin(turning)
    return jnp.sum(fading * wave, axis=1)


def channel_block(pieces, tables):
    grouped, taps_part, decay_part, freq_part, coef_part, skip_part = pieces
    query, keys_part, values_part = (grouped[0], grouped[1], grouped[2])
    length = keys_part.shape[-1]
    taps_real, taps_imag = kernel_spectrum(taps_part, 2 * length, tables)
    shifted = causal_conv(keys_part, taps_real, taps_imag, tables)
    product = shifted * values_part
    kernel = mode_kernel(decay_part, freq_part, coef_part, length)
    kern_real, kern_imag = kernel_spectrum(kernel, 2 * length, tables)
    state_out = (
        causal_conv(product, kern_real, kern_imag, tables) + skip_part[:, None, None] * product
    )
    return query * state_out


def channel_mixer(grouped_all, taps, rates, freqs, coefs, skips, tables):
    channels = taps.shape[0]
    group_width = math.gcd(channels, 8)
    group_count = channels // group_width
    stacked = grouped_all.reshape((3, group_count, group_width) + grouped_all.shape[2:]).transpose(
        1, 0, 2, 3, 4
    )

    def one_group(pieces):
        return channel_block(pieces, tables)

    results = lax.map(
        jax.checkpoint(one_group),
        (
            stacked,
            taps.reshape(group_count, group_width, -1),
            rates.reshape(group_count, group_width, -1),
            freqs.reshape(group_count, group_width, -1),
            coefs.reshape(group_count, group_width, 2, -1),
            skips.reshape(group_count, group_width),
        ),
    )
    return results.reshape((channels,) + results.shape[2:])


def arrange_slots(received, slot_row, slot_live):
    picked = jnp.take(received, slot_row, axis=0)
    live_shape = slot_live.reshape((-1,) + (1,) * (received.ndim - 1))
    return jnp.where(live_shape, picked, jnp.zeros_like(picked))


def local(
    tokens,
    cotangent,
    lengths,
    norm_gains,
    shift_taps,
    decay_rate,
    frequency,
    mode_coef,
    skip_gain,
    qkv_weight,
    out_weight,
    up_weight,
    down_weight,
):
    parts = lax.axis_size("seq")
    group = lax.axis_index("dp")
    position = lax.axis_index("seq")
    slot_count, part_length, width = tokens.shape
    block_count = SLOT // BLK
    per_part = block_count // parts
    blocks_dev = slot_count * per_part
    pair_count = blocks_dev // parts
    valid_dev = 5 * block_count * slot_count // (8 * parts)
    channels = width // parts
    row_total = valid_dev * BLK
    group_lengths = lax.dynamic_slice_in_dim(lengths, group * slot_count, slot_count, 0)
    needed = (group_lengths + BLK - 1) // BLK
    block_ids = jnp.arange(block_count, dtype=jnp.int32)
    filled = (block_ids[None, :] < needed[:, None]).astype(jnp.int32)
    source_fill = (
        filled.reshape(slot_count, parts, per_part).transpose(1, 0, 2).reshape(parts, blocks_dev)
    )
    valid_count = jnp.sum(source_fill, axis=1)
    offsets = jnp.cumsum(valid_count) - valid_count
    rank_valid = jnp.cumsum(source_fill, axis=1) - 1
    rank_empty = valid_count[:, None] + jnp.cumsum(1 - source_fill, axis=1) - 1
    ranking = jnp.where(source_fill == 1, rank_valid, rank_empty)
    rank_ids = jnp.arange(blocks_dev, dtype=jnp.int32)[None, :]
    target = (offsets[:, None] + rank_ids) % parts
    empty = rank_ids >= valid_count[:, None]
    target_hot = (target[:, :, None] == jnp.arange(parts, dtype=jnp.int32)[None, None, :]).astype(
        jnp.int32
    )
    empty_hot = (target_hot * empty[:, :, None].astype(jnp.int32)).reshape(
        parts * blocks_dev, parts
    )
    earlier = (jnp.cumsum(empty_hot, axis=0) - empty_hot).reshape(parts, blocks_dev, parts)
    earlier_own = jnp.sum(earlier * target_hot, axis=2)
    landing = jnp.where(empty, valid_dev + earlier_own, (offsets[:, None] + rank_ids) // parts)
    entry_by_rank = target * blocks_dev + landing
    entries = jnp.take_along_axis(entry_by_rank, ranking, axis=1)
    slot_entry = (
        entries.reshape(parts, slot_count, per_part)
        .transpose(1, 0, 2)
        .reshape(slot_count * block_count)
    )
    owner_of = (
        jnp.zeros((parts * blocks_dev,), jnp.int32)
        .at[slot_entry]
        .set(jnp.arange(slot_count * block_count, dtype=jnp.int32))
    )
    send_order = jnp.argsort(entries, axis=1)
    sorted_entries = jnp.take_along_axis(entries, send_order, axis=1)
    my_order = lax.dynamic_index_in_dim(send_order, position, 0, keepdims=False)
    arrival_pos = (
        lax.dynamic_slice_in_dim(sorted_entries, position * pair_count, pair_count, 1)
        - position * blocks_dev
    ).reshape(blocks_dev)
    arrival_index = (
        jnp.zeros((blocks_dev,), jnp.int32)
        .at[arrival_pos]
        .set(jnp.arange(blocks_dev, dtype=jnp.int32))
    )
    home_index = (
        jnp.zeros((blocks_dev,), jnp.int32)
        .at[my_order]
        .set(jnp.arange(blocks_dev, dtype=jnp.int32))
    )
    token_blocks = jnp.take(tokens.reshape(blocks_dev, BLK, width), my_order, axis=0).reshape(
        parts, pair_count * BLK, width
    )
    cot_blocks = jnp.take(cotangent.reshape(blocks_dev, BLK, width), my_order, axis=0).reshape(
        parts, pair_count * BLK, width
    )
    sent_tokens, sent_cot = (
        lax.all_to_all(token_blocks, "seq", split_axis=0, concat_axis=0, tiled=True),
        lax.all_to_all(cot_blocks, "seq", split_axis=0, concat_axis=0, tiled=True),
    )
    keep_index = arrival_index[:valid_dev]
    dealt_tokens = jnp.take(sent_tokens.reshape(blocks_dev, BLK, width), keep_index, axis=0)
    dealt_cot = jnp.take(sent_cot.reshape(blocks_dev, BLK, width), keep_index, axis=0)
    dealt_owner = lax.dynamic_slice_in_dim(owner_of, position * blocks_dev, valid_dev, 0)
    slot_of = dealt_owner // block_count
    start_of = dealt_owner % block_count * BLK
    inside = (
        start_of[:, None] + jnp.arange(BLK, dtype=jnp.int32)[None, :]
        < jnp.take(group_lengths, slot_of)[:, None]
    )
    live_mask = inside.astype(jnp.float32).reshape(row_total, 1)
    gains_all, taps_all, rates_all, freqs_all, coefs_all, skips_all = (
        lax.all_gather(norm_gains, ("dp", "seq"), axis=0, tiled=True),
        lax.all_gather(shift_taps, ("dp", "seq"), axis=0, tiled=True),
        lax.all_gather(decay_rate, ("dp", "seq"), axis=0, tiled=True),
        lax.all_gather(frequency, ("dp", "seq"), axis=0, tiled=True),
        lax.all_gather(mode_coef, ("dp", "seq"), axis=0, tiled=True),
        lax.all_gather(skip_gain, ("dp", "seq"), axis=0, tiled=True),
    )
    qkv_full, out_full = (
        lax.all_gather(qkv_weight, ("dp", "seq"), axis=0, tiled=True),
        lax.all_gather(out_weight, ("dp", "seq"), axis=0, tiled=True),
    )
    input_rows = dealt_tokens.reshape(row_total, width).astype(jnp.float32)
    normed_one, norm_one_back = jax.vjp(layer_norm, input_rows, gains_all[:, 0])
    normed_low = normed_one.astype(jnp.bfloat16)
    projected = mat_dot(normed_low, qkv_full, ((1,), (0,))).astype(jnp.bfloat16)
    spread_qkv = lax.all_to_all(
        projected.reshape(valid_dev, BLK, 3, width), "seq", split_axis=3, concat_axis=0, tiled=True
    )
    slot_source = slot_entry // blocks_dev
    slot_place = slot_entry % blocks_dev
    slot_live = slot_place < valid_dev
    slot_row = jnp.where(slot_live, slot_source * valid_dev + slot_place, 0)
    channel_qkv = (
        arrange_slots(spread_qkv, slot_row, slot_live)
        .reshape(slot_count, SLOT, 3, channels)
        .transpose(2, 3, 0, 1)
        .astype(jnp.float32)
    )
    channel_start = position * channels

    def local_slice(values):
        return lax.dynamic_slice_in_dim(values, channel_start, channels, 0)

    tables = dft_tables(2 * SLOT)

    def mixer_local(grouped_all, taps, rates, freqs, coefs, skips):
        return channel_mixer(grouped_all, taps, rates, freqs, coefs, skips, tables)

    mixed_channels, mixer_back = jax.vjp(
        mixer_local,
        channel_qkv,
        local_slice(taps_all),
        local_slice(rates_all),
        local_slice(freqs_all),
        local_slice(coefs_all),
        local_slice(skips_all),
    )
    mixed_low = mixed_channels.astype(jnp.bfloat16)
    source_blocks = owner_of.reshape(parts, blocks_dev)[:, :valid_dev]
    mixed_blocks = mixed_low.transpose(1, 2, 0).reshape(slot_count * block_count, BLK, channels)
    mixed_rows = lax.all_to_all(
        jnp.take(mixed_blocks, source_blocks, axis=0),
        "seq",
        split_axis=0,
        concat_axis=3,
        tiled=True,
    ).reshape(row_total, width)
    hidden = input_rows + mat_dot(mixed_rows, out_full, ((1,), (0,)))
    up_full, down_full = (
        lax.all_gather(up_weight, ("dp", "seq"), axis=0, tiled=True),
        lax.all_gather(down_weight, ("dp", "seq"), axis=0, tiled=True),
    )
    normed_two, norm_two_back = jax.vjp(layer_norm, hidden, gains_all[:, 1])
    normed_two_low = normed_two.astype(jnp.bfloat16)
    pre_act = mat_dot(normed_two_low, up_full, ((1,), (0,)))
    activity, gelu_back = jax.vjp(exact_gelu, pre_act)
    activity_low = activity.astype(jnp.bfloat16)
    result_rows = live_mask * (hidden + mat_dot(activity_low, down_full, ((1,), (0,))))
    up_back, down_back = (
        lax.all_gather(up_weight, ("dp", "seq"), axis=0, tiled=True),
        lax.all_gather(down_weight, ("dp", "seq"), axis=0, tiled=True),
    )
    grad_sum = live_mask * dealt_cot.reshape(row_total, width).astype(jnp.float32)
    grad_branch = grad_sum.astype(jnp.bfloat16)
    down_grad = mat_dot(activity_low, grad_branch, ((0,), (0,)))
    grad_act = mat_dot(grad_branch, down_back, ((1,), (1,)))
    grad_pre = gelu_back(grad_act)[0].astype(jnp.bfloat16)
    up_grad = mat_dot(normed_two_low, grad_pre, ((0,), (0,)))
    grad_normed = mat_dot(grad_pre, up_back, ((1,), (1,)))
    grad_hidden_norm, grad_gain_two = norm_two_back(grad_normed)
    grad_hidden = grad_sum + grad_hidden_norm
    up_share, down_share, gain_two_share = (
        lax.psum_scatter(up_grad, ("dp", "seq"), scatter_dimension=0, tiled=True),
        lax.psum_scatter(down_grad, ("dp", "seq"), scatter_dimension=0, tiled=True),
        lax.psum_scatter(grad_gain_two, ("dp", "seq"), scatter_dimension=0, tiled=True),
    )
    qkv_back, out_back = (
        lax.all_gather(qkv_weight, ("dp", "seq"), axis=0, tiled=True),
        lax.all_gather(out_weight, ("dp", "seq"), axis=0, tiled=True),
    )
    grad_mix = grad_hidden.astype(jnp.bfloat16)
    out_grad = mat_dot(mixed_rows, grad_mix, ((0,), (0,)))
    grad_mixed = mat_dot(grad_mix, out_back, ((1,), (1,))).astype(jnp.bfloat16)
    spread_grad = lax.all_to_all(
        grad_mixed.reshape(valid_dev, BLK, width), "seq", split_axis=2, concat_axis=0, tiled=True
    )
    channel_grad = (
        arrange_slots(spread_grad, slot_row, slot_live)
        .reshape(slot_count, SLOT, channels)
        .transpose(2, 0, 1)
        .astype(jnp.float32)
    )
    grad_qkv_c, grad_taps, grad_rates, grad_freqs, grad_coefs, grad_skips = mixer_back(channel_grad)
    grad_qkv_blocks = (
        grad_qkv_c.astype(jnp.bfloat16)
        .transpose(2, 3, 0, 1)
        .reshape(slot_count * block_count, BLK, 3, channels)
    )
    grad_projected = lax.all_to_all(
        jnp.take(grad_qkv_blocks, source_blocks, axis=0),
        "seq",
        split_axis=0,
        concat_axis=4,
        tiled=True,
    ).reshape(row_total, 3 * width)
    qkv_grad = mat_dot(normed_low, grad_projected, ((0,), (0,)))
    grad_normed_one = mat_dot(grad_projected, qkv_back, ((1,), (1,)))
    grad_input_norm, grad_gain_one = norm_one_back(grad_normed_one)
    grad_input = grad_hidden + grad_input_norm

    def widen(values):
        holder = jnp.zeros((width,) + values.shape[1:], jnp.float32)
        return lax.dynamic_update_slice_in_dim(holder, values, channel_start, 0)

    shares = (
        lax.psum_scatter(qkv_grad, ("dp", "seq"), scatter_dimension=0, tiled=True),
        lax.psum_scatter(out_grad, ("dp", "seq"), scatter_dimension=0, tiled=True),
        lax.psum_scatter(grad_gain_one, ("dp", "seq"), scatter_dimension=0, tiled=True),
        lax.psum_scatter(widen(grad_taps), ("dp", "seq"), scatter_dimension=0, tiled=True),
        lax.psum_scatter(widen(grad_rates), ("dp", "seq"), scatter_dimension=0, tiled=True),
        lax.psum_scatter(widen(grad_freqs), ("dp", "seq"), scatter_dimension=0, tiled=True),
        lax.psum_scatter(widen(grad_coefs), ("dp", "seq"), scatter_dimension=0, tiled=True),
        lax.psum_scatter(widen(grad_skips), ("dp", "seq"), scatter_dimension=0, tiled=True),
    )
    padding = jnp.zeros((blocks_dev - valid_dev, BLK, width), jnp.float32)
    full_result = jnp.concatenate([result_rows.reshape(valid_dev, BLK, width), padding], axis=0)
    full_grad = jnp.concatenate([grad_input.reshape(valid_dev, BLK, width), padding], axis=0)
    back_result, back_grad = (
        lax.all_to_all(
            jnp.take(full_result, arrival_pos, axis=0)
            .reshape(parts, pair_count * BLK, width)
            .astype(jnp.bfloat16),
            "seq",
            split_axis=0,
            concat_axis=0,
            tiled=True,
        ).astype(jnp.float32),
        lax.all_to_all(
            jnp.take(full_grad, arrival_pos, axis=0)
            .reshape(parts, pair_count * BLK, width)
            .astype(jnp.bfloat16),
            "seq",
            split_axis=0,
            concat_axis=0,
            tiled=True,
        ).astype(jnp.float32),
    )
    layer_out = (
        jnp.take(back_result.reshape(blocks_dev, BLK, width), home_index, axis=0)
        .reshape(slot_count, part_length, width)
        .astype(jnp.bfloat16)
    )
    input_grad = jnp.take(back_grad.reshape(blocks_dev, BLK, width), home_index, axis=0).reshape(
        slot_count, part_length, width
    )
    gains_grad = jnp.stack([shares[2], gain_two_share], axis=1)
    return (
        layer_out,
        input_grad,
        gains_grad,
        shares[3],
        shares[4],
        shares[5],
        shares[6],
        shares[7],
        shares[0],
        shares[1],
        up_share,
        down_share,
    )


def solution(mesh):
    return jax.shard_map(
        local,
        mesh=mesh,
        in_specs=(
            P("dp", "seq", None),
            P("dp", "seq", None),
            P(),
            P(("dp", "seq"), None),
            P(("dp", "seq"), None),
            P(("dp", "seq"), None),
            P(("dp", "seq"), None),
            P(("dp", "seq"), None, None),
            P(("dp", "seq")),
            P(("dp", "seq"), None),
            P(("dp", "seq"), None),
            P(("dp", "seq"), None),
            P(("dp", "seq"), None),
        ),
        out_specs=(
            P("dp", "seq", None),
            P("dp", "seq", None),
            P(("dp", "seq"), None),
            P(("dp", "seq"), None),
            P(("dp", "seq"), None),
            P(("dp", "seq"), None),
            P(("dp", "seq"), None, None),
            P(("dp", "seq")),
            P(("dp", "seq"), None),
            P(("dp", "seq"), None),
            P(("dp", "seq"), None),
            P(("dp", "seq"), None),
        ),
        check_vma=False,
    )
```

profile of v0, /device:TPU:0, one launch (start us, length us, event | category | flops | bytes accessed | tf_op | source)
XLA Modules:
  0.0 4122.6 jit_solution(13538098245507924563)
XLA Ops:
  26.0 56.9 %all-gather = f32[32,24,2]{1,2,0:T(2,128)S(1)} all-gather(f32[1,24,2]{1,2,0:T(2,128)S(1)} %bitcast.1099), channel_id=1, replica_groups=mesh['dp'=8,'seq'=4] {'dp','seq'}, dimensions={0}, use_global_device_ids=true | all-gather | bytes 6336 | tf_op jit(solution)/shard_map/all_gather | solution.py:281
  101.6 13.3 copy.499
  129.6 68.8 %all-reduce.17 = f32[768]{0:T(1024)S(1)} all-reduce(f32[768]{0:T(1024)S(1)} %dynamic-update-slice), channel_id=1, replica_groups=mesh['dp'=8,'seq'=4] {'dp','seq'}, use_global_device_ids=true, to_apply=%add.17 | all-reduce | flops 768 | bytes 6144
  198.5 44.3 %all_gather.38 = f32[768,2,32]{2,1,0:T(2,128)S(1)} all-gather(f32[24,2,32]{2,1,0:T(2,128)S(1)} %copy-done.61), channel_id=1, replica_groups=mesh['dp'=8,'seq'=4] {'dp','seq'}, dimensions={0}, use_global_device_ids=true | all-gather | bytes 202752 | tf_op jit(solution)/shard_map/all_gather | solution.py:285
  243.8 38.4 all_gather.39
  282.3 38.7 all_gather.37
  321.0 38.0 all_gather.36
  375.4 13.1 copy.501
  403.4 11.6 copy.503
  423.8 991.8 %while.40 = (s32[]{:T(128)}, bf16[24,8,2,2048]{3,1,0,2:T(8,128)(2,1)}, f32[24,3,8,2,2048]{4,2,3,1,0:T(8,128)}, f32[24,8,64]{2,1,0:T(8,128)}, f32[24,8,32]{2,1,0:...) while((s32[]{:T(128)}, ...), condition=%wide.region_13.17_spmd.clone.clone, body=%wide.region_11.16_spmd.clone.clone.sunk | while | flops 1522780416 | bytes 34052900 | solution.py:160
  1432.4 11.4 all-to-all-done.2
  1462.5 24.3 add_convert_fusion
  1506.4 13.8 all-to-all-done.5
  1544.6 1630.9 %while.39 = (s32[]{:T(128)}, bf16[24,3,8,2,2048]{4,2,0,3,1:T(8,128)(2,1)}, f32[24,8,64]{2,1,0:T(8,128)}, f32[24,8,32]{2,1,0:T(8,128)}, f32[24,8,32]{2,1,0:T(8,12...) while((s32[]{:T(128)}, ...), condition=%wide.region_34.39_spmd.clone, body=%wide.region_19.38_spmd.clone.sunk | while | flops 3047847936 | bytes 84003480 | solution.py:160
  1600.0 10.8 fusion.1047
  1666.7 10.8 fusion.1047
  1733.3 10.8 fusion.1047
  1800.0 10.8 fusion.1047
  1866.6 10.8 fusion.1047
  1933.3 10.8 fusion.1047
  2000.0 10.8 fusion.1047
  2066.6 10.8 fusion.1047
  2133.3 10.8 fusion.1047
  3213.4 45.3 %all-to-all-done.6 = bf16[4,10,64,3,192]{4,2,3,1,0:T(8,128)(2,1)} async-done(((bf16[4,10,64,3,192]{4,2,3,1,0:T(8,128)(2,1)}), bf16[4,10,64,3,192]{4,2,3,1,0:T(8,128)(2,1)}, u32[]{:S(2)}, u32[]{:S(2)}) %all-to-all-start.6) | async-done | bytes 2949152 | tf_op jit(solution)/shard_map/all_to_all | solution.py:389
  3333.5 23.2 all_to_all.86
  3363.7 49.1 %all-reduce.25 = (f32[768]{0:T(1024)S(1)}, f32[768]{0:T(1024)S(1)}, f32[768]{0:T(1024)S(1)}) all-reduce(f32[768]{0:T(1024)S(1)} %copy-done.72, f32[768]{0:T(1024)S(1)} %get-tuple-element.1178, f32[768]{0:T(1024)S(1)} %dynamic_update_slice.85), channel_id=3, replica_groups=mesh['dp'=8,'seq'=4] {'dp','seq'}, use_global_device_ids=true, to_apply=%region_40.45.clone | all-reduce | flops 2304 | bytes 18432
  3425.1 77.7 %reduce-scatter.26.cloned.1.call-done = f32[24,32]{1,0:T(8,128)} async-done(((f32[768,32]{1,0:T(8,128)}), f32[24,32]{1,0:T(8,128)}) %reduce-scatter.26.cloned.1.call-update) | async-done | bytes 3088
  3502.7 100.2 %reduce-scatter.22.cloned.1.call-done = f32[24,64]{1,0:T(8,128)} async-done(((f32[768,64]{1,0:T(8,128)}), f32[24,64]{1,0:T(8,128)}) %reduce-scatter.22.cloned.1.call-update) | async-done | bytes 6160
  3602.9 104.0 %reduce-scatter.16.cloned.1.call-done = f32[24,768]{1,0:T(8,128)} async-done(((f32[768,768]{1,0:T(8,128)}), f32[24,768]{1,0:T(8,128)}) %reduce-scatter.16.cloned.1.call-update) | async-done | bytes 73744 | tf_op jit(solution)/shard_map/reduce_scatter | solution.py:407
  3707.0 125.2 %reduce-scatter.14.cloned.1.call-done = f32[24,2304]{1,0:T(8,128)} async-done(((f32[768,2304]{1,0:T(8,128)}), f32[24,2304]{1,0:T(8,128)}) %reduce-scatter.14.cloned.1.call-update) | async-done | bytes 221200 | tf_op jit(solution)/shard_map/reduce_scatter | solution.py:406
  3832.2 141.3 %reduce-scatter.18.cloned.1.call-done = f32[24,3072]{1,0:T(8,128)} async-done(((f32[768,3072]{1,0:T(8,128)}), f32[24,3072]{1,0:T(8,128)}) %reduce-scatter.18.cloned.1.call-update) | async-done | bytes 294928 | tf_op jit(solution)/shard_map/reduce_scatter | solution.py:363
  3973.5 141.9 %reduce-scatter.20.cloned.1.call-done = f32[96,768]{1,0:T(8,128)} async-done(((f32[3072,768]{1,0:T(8,128)}), f32[96,768]{1,0:T(8,128)}) %reduce-scatter.20.cloned.1.call-update) | async-done | bytes 294928 | tf_op jit(solution)/shard_map/reduce_scatter | solution.py:364
  (5264 shorter events, 2752.7 us)
Async XLA Ops:
  7.2 80.8 %all-gather.6.cloned.1.call-start = ((), (), s32[]{:S(2)}) async-start(), calls=%async_computation.15 | async-start | bytes 3649536 | tf_op jit(solution)/shard_map/all_gather | solution.py:289
  7.9 1440.8 %all-gather.8.cloned.1.call-start = ((), (), s32[]{:S(2)}) async-start(), calls=%async_computation.16 | async-start | bytes 1216512 | tf_op jit(solution)/shard_map/all_gather | solution.py:290
  8.7 1444.4 %all-gather.10.cloned.1.call-start = ((), (), s32[]{:S(2)}) async-start(), calls=%async_computation.17 | async-start | bytes 4866048 | tf_op jit(solution)/shard_map/all_gather | solution.py:340
  21.6 63.2 %all-to-all-start = ((bf16[4,256,768]{2,1,0:T(8,128)(2,1)}), bf16[4,256,768]{2,1,0:T(8,128)(2,1)S(1)}, u32[]{:S(2)}, u32[]{:S(2)}) async-start(bf16[4,256,768]{2,1,0:T(8,128)(2,1)} %bitcast.11), calls=%async_computation | async-start | bytes 3145728 | tf_op jit(solution)/shard_map/all_to_all | solution.py:266
  84.8 1406.1 %copy-start.38 = (f32[768]{0:T(1024)}, f32[768]{0:T(1024)S(1)}, u32[]{:S(2)}) copy-start(f32[768]{0:T(1024)S(1)} %get-tuple-element.1180) | copy-start | bytes 9220
  86.4 1362.3 %copy-start.3 = (bf16[10,64,768]{2,1,0:T(8,128)(2,1)}, bf16[10,64,768]{2,1,0:T(8,128)(2,1)S(1)}, u32[]{:S(2)}) copy-start(bf16[10,64,768]{2,1,0:T(8,128)(2,1)S(1)} %get-tuple-element.1239) | copy-start | bytes 2949124
  123.2 75.3 %copy-start.61 = (f32[24,2,32]{2,1,0:T(2,128)S(1)}, f32[24,2,32]{2,1,0:T(2,128)}, u32[]{:S(2)}) copy-start(f32[24,2,32]{2,1,0:T(2,128)} %param.32) | copy-start | bytes 18436
  123.2 239.7 %all-to-all-start.1 = ((bf16[4,2,184320]{2,1,0:T(2,128)(2,1)}), bf16[4,2,184320]{2,1,0:T(2,128)(2,1)}, u32[]{:S(2)}, u32[]{:S(2)}) async-start(bf16[4,2,184320]{2,1,0:T(2,128)(2,1)} %reshape.1408), calls=%async_computation.1 | async-start | bytes 5898240 | tf_op jit(solution)/shard_map/all_to_all | solution.py:296
  128.0 115.8 %copy-start.64 = (f32[24,32]{1,0:T(8,128)S(1)}, f32[24,32]{1,0:T(8,128)}, u32[]{:S(2)}) copy-start(f32[24,32]{1,0:T(8,128)} %param.31) | copy-start | bytes 9220
  128.0 154.2 %copy-start.65 = (f32[24,32]{1,0:T(8,128)S(1)}, f32[24,32]{1,0:T(8,128)}, u32[]{:S(2)}) copy-start(f32[24,32]{1,0:T(8,128)} %param.30) | copy-start | bytes 9220
  128.0 193.0 %copy-start.66 = (f32[24,64]{1,0:T(8,128)S(1)}, f32[24,64]{1,0:T(8,128)}, u32[]{:S(2)}) copy-start(f32[24,64]{1,0:T(8,128)} %param.29) | copy-start | bytes 18436
  128.0 230.9 %copy-start.69 = (s32[2]{0:T(128)S(1)}, s32[2]{0:T(128)}, u32[]{:S(2)}) copy-start(s32[2]{0:T(128)} %get-tuple-element.1247) | copy-start | bytes 28
  128.1 1334.4 %all-gather.12.cloned.1.call-start = ((), (), s32[]{:S(2)}) async-start(), calls=%async_computation.18 | async-start | bytes 4866048 | tf_op jit(solution)/shard_map/all_gather | solution.py:341
  129.1 268.5 %copy-start.46 = (pred[2,2048]{1,0:T(4,128)(4,1)}, pred[2,2048]{1,0:T(4,128)(4,1)S(1)}, u32[]{:S(2)}) copy-start(pred[2,2048]{1,0:T(4,128)(4,1)S(1)} %broadcast_in_dim.360) | copy-start | bytes 12292
  129.3 268.3 %copy-start.48 = (pred[2,2048]{1,0:T(4,128)(4,1)}, pred[2,2048]{1,0:T(4,128)(4,1)S(1)}, u32[]{:S(2)}) copy-start(pred[2,2048]{1,0:T(4,128)(4,1)S(1)} %broadcast_in_dim.363) | copy-start | bytes 12292
  361.0 1058.4 %copy-start.62 = (s32[1024]{0:T(1024)}, s32[1024]{0:T(1024)S(1)}, u32[]{:S(2)}) copy-start(s32[1024]{0:T(1024)S(1)} %pad_clamp_fusion.2) | copy-start | bytes 12292
  362.9 1058.8 %copy-start.70 = (pred[4,10]{1,0:T(4,128)(4,1)}, pred[4,10]{1,0:T(4,128)(4,1)S(1)}, u32[]{:S(2)}) copy-start(pred[4,10]{1,0:T(4,128)(4,1)S(1)} %compare_and_fusion.5) | copy-start | bytes 124
  362.9 1060.0 %all-to-all-start.4 = ((bf16[4,256,768]{2,1,0:T(8,128)(2,1)}), bf16[4,256,768]{2,1,0:T(8,128)(2,1)}, u32[]{:S(2)}, u32[]{:S(2)}) async-start(bf16[4,256,768]{2,1,0:T(8,128)(2,1)} %bitcast.39), calls=%async_computation.4 | async-start | bytes 3145728 | tf_op jit(solution)/shard_map/all_to_all | solution.py:267
  1422.9 20.9 all-to-all-start.2
  1426.7 65.0 %copy-start.54 = (f32[640]{0:T(1024)}, f32[640]{0:T(1024)S(1)}, u32[]{:S(2)}) copy-start(f32[640]{0:T(1024)S(1)} %reshape.1136) | copy-start | bytes 7684
  1502.1 18.1 all-to-all-start.5
  1506.4 1856.0 %all-reduce.28.cloned.1.call-start = ((), (), s32[]{:S(2)}) async-start(), calls=%async_computation.23 | async-start | bytes 1572864
  3177.8 247.2 %reduce-scatter.24.cloned.1.call-start = ((), (), s32[]{:S(2)}) async-start(), calls=%async_computation.25 | async-start | bytes 405504
  3178.7 324.0 %reduce-scatter.26.cloned.1.call-start = ((), (), s32[]{:S(2)}) async-start(), calls=%async_computation.26 | async-start | bytes 405504
  3179.6 423.3 %reduce-scatter.22.cloned.1.call-start = ((), (), s32[]{:S(2)}) async-start(), calls=%async_computation.24 | async-start | bytes 405504
  3180.5 526.5 %reduce-scatter.16.cloned.1.call-start = ((), (), s32[]{:S(2)}) async-start(), calls=%async_computation.20 | async-start | bytes 2433024 | tf_op jit(solution)/shard_map/reduce_scatter | solution.py:407
  3208.0 50.7 %all-to-all-start.6 = ((bf16[4,10,64,3,192]{4,2,3,1,0:T(8,128)(2,1)}), bf16[4,10,64,3,192]{4,2,3,1,0:T(8,128)(2,1)}, u32[]{:S(2)}, u32[]{:S(2)}) async-start(bf16[4,10,64,3,192]{4,2,3,1,0:T(8,128)(2,1)} %broadcast_select_fusion), calls=%async_computation.6 | async-start | bytes 7864320 | tf_op jit(solution)/shard_map/all_to_all | solution.py:389
  3212.9 619.3 %reduce-scatter.14.cloned.1.call-start = ((), (), s32[]{:S(2)}) async-start(), calls=%async_computation.19 | async-start | bytes 7299072 | tf_op jit(solution)/shard_map/reduce_scatter | solution.py:406
  3280.1 693.4 %reduce-scatter.18.cloned.1.call-start = ((), (), s32[]{:S(2)}) async-start(), calls=%async_computation.21 | async-start | bytes 9732096 | tf_op jit(solution)/shard_map/reduce_scatter | solution.py:363
  3290.4 825.0 %reduce-scatter.20.cloned.1.call-start = ((), (), s32[]{:S(2)}) async-start(), calls=%async_computation.22 | async-start | bytes 9732096 | tf_op jit(solution)/shard_map/reduce_scatter | solution.py:364
  3356.7 61.6 %all-to-all-start.3 = ((bf16[4,256,768]{2,1,0:T(8,128)(2,1)}), bf16[4,256,768]{2,1,0:T(8,128)(2,1)}, u32[]{:S(2)}, u32[]{:S(2)}) async-start(bf16[4,256,768]{2,1,0:T(8,128)(2,1)} %bitcast.35), calls=%async_computation.3 | async-start | bytes 3145728 | tf_op jit(solution)/shard_map/all_to_all | solution.py:419
  3420.4 695.0 %copy-start.1 = (bf16[2,512,768]{2,1,0:T(8,128)(2,1)S(1)}, bf16[2,512,768]{2,1,0:T(8,128)(2,1)}, u32[]{:S(2)}) copy-start(bf16[2,512,768]{2,1,0:T(8,128)(2,1)} %param.25) | copy-start | bytes 4718596
  (275 other events, 1479.2 us)
Sparse Core Ops, SparseCore 0:
  10.9 65.0 all-gather.5
  78.9 52.8 all-gather.7
  134.7 62.5 all-gather.9
  200.1 64.8 all-gather.11
  3177.9 125.2 all-reduce.27
  3309.4 93.8 reduce-scatter.23
  3408.8 93.9 reduce-scatter.25
  3509.0 93.8 reduce-scatter.21
  3608.8 98.1 reduce-scatter.15
  3714.0 118.1 reduce-scatter.13
  3838.7 134.8 reduce-scatter.17
  3980.9 134.4 reduce-scatter.19
where the time goes:
time: 4140 us; the launch traced here: 4120 us
  matrix products  1480 us (36%)
  waiting for transfers between devices  764 us (18%)
  local copies, waits for them, and re-layouts  707 us (17%)
  other arithmetic  695 us (17%)
  blocking collectives  357 us (9%)
  loops' own time  75.8 us (2%)
    dot_general x288, matrix products, forward_dft(): jnp.einsum('kn,...nm->...km', sin_first, shaped, precision=highest)  295 us
    dot_general x288, matrix products, forward_dft(): jnp.einsum('kn,...nm->...km', cos_first, shaped, precision=highest)  295 us
    reduce_sum x24, other arithmetic, mode_kernel(): coef_part[:, 1, :, None] * jnp.sin(turning)  260 us
    reduce_sum x24, other arithmetic, mode_kernel(): return jnp.sum(fading * wave, axis=1)  206 us
    unnamed x16, waiting for transfers between devices  181 us
    squeeze x216, local copies, waits for them, and re-layouts, channel_mixer(): lax.map(jax.checkpoint(one_group), (stacked, taps.reshape(group_count, gr...  150 us
    reduce_scatter x1, waiting for transfers between devices, local(): lax.psum_scatter(down_grad, ('dp', 'seq'), scatter_dimension=0, tiled=True)  142 us
    reduce_scatter x1, waiting for transfers between devices, local(): lax.psum_scatter(up_grad, ('dp', 'seq'), scatter_dimension=0, tiled=True)  141 us

commit v1 on v0

v1 whole, which is shorter than its diff:
```python
import functools

import jax
import jax.numpy as jnp
import numpy as np
from jax import lax
from jax.experimental import pallas as pl
from jax.experimental.pallas import tpu as pltpu
from jax.sharding import PartitionSpec as P

SLOT = 2048
FINE = 64
highest = lax.Precision.HIGHEST
both = ("dp", "seq")


def layer_norm(row_block, gain):
    center = row_block - jnp.mean(row_block, axis=-1, keepdims=True)
    spread = jnp.mean(center * center, axis=-1, keepdims=True)
    return center * lax.rsqrt(spread + 1e-05) * gain


def exact_gelu(values):
    return jax.nn.gelu(values, approximate=False)


def mat_dot(left, right, contract):
    return lax.dot_general(left, right, (contract, ((), ())), preferred_element_type=jnp.float32)


def wave_table(step):
    order = np.concatenate([np.arange(0, step, 2), np.arange(1, step, 2)])
    turns = (2 * order[:, None] + 1) * np.arange(step)[None, :] % (4 * step)
    angles = turns * (np.pi / (2 * step))
    return np.concatenate([np.cos(angles), -np.sin(angles)], axis=0)


def lanes(index, width):
    return slice(index * width, (index + 1) * width)


def transform(table_ref, source_ref, target_ref):
    rows = target_ref.shape[0]
    chunk = min(rows, 256)

    @pl.loop(0, rows // chunk)
    def _(index):
        window = pl.ds(pl.multiple_of(index * chunk, chunk), chunk)
        target_ref[window, :] = jnp.dot(
            table_ref[window, :], source_ref[...], preferred_element_type=jnp.float32
        ).astype(target_ref.dtype)


def over_bins(step, body):
    chunk = 16
    for half, sign in ((0, 1.0), (1, -1.0)):

        @pl.loop(0, step // (2 * chunk))
        def _(index):
            start = pl.multiple_of(half * (step // 2) + index * chunk, chunk)
            body(sign, pl.ds(start, chunk), pl.ds(pl.multiple_of(step + start, chunk), chunk))


def times(left, right):
    return (left[0] * right[0] - left[1] * right[1], left[0] * right[1] + left[1] * right[0])


def times_conj(left, right):
    return (left[0] * right[0] + left[1] * right[1], left[0] * right[1] - left[1] * right[0])


def plus(left, right):
    return right if left is None else (left[0] + right[0], left[1] + right[1])


def load_bins(ref, real, imag, count, width):
    return [
        (
            ref[real, lanes(i, width)].astype(jnp.float32),
            ref[imag, lanes(i, width)].astype(jnp.float32),
        )
        for i in range(count)
    ]


def store_bins(ref, real, imag, index, width, value):
    ref[real, lanes(index, width)] = value[0].astype(ref.dtype)
    ref[imag, lanes(index, width)] = value[1].astype(ref.dtype)


def with_last(bins, sign):
    out = [bins[0]]
    for before, now in zip(bins[:-1], bins[1:]):
        out.append((now[0] - sign * before[1], now[1] + sign * before[0]))
    return out


def with_next(bins, sign):
    out = []
    for now, after in zip(bins[:-1], bins[1:]):
        out.append((now[0] + sign * after[1], now[1] - sign * after[0]))
    return out + [bins[-1]]


def mix_forward(
    count, step, width,
    table_ref, inverse_ref, query_ref, keys_ref, values_ref, kernel_ref, taps_ref, skip_ref,
    mixed_ref, shifted_ref, state_ref, keys_hat_ref, product_hat_ref, kernel_hat_ref, taps_hat_ref,
    source_ref, spectrum_ref, scaled_ref,
):
    state_taps = taps_ref.shape[0]
    chunk = min(step, 128)
    for i in range(count):
        source_ref[:, lanes(i, width)] = keys_ref[pl.ds(i * step, step), :]
    transform(table_ref, source_ref, spectrum_ref)
    taps_hat_ref[...] = jnp.dot(
        table_ref[:, :state_taps], taps_ref[...], preferred_element_type=jnp.float32
    )

    def shift_bins(sign, real, imag):
        keys = load_bins(spectrum_ref, real, imag, count, width)
        taps = (taps_hat_ref[real, :], taps_hat_ref[imag, :])
        for i, value in enumerate(with_last(keys, sign)):
            store_bins(keys_hat_ref, real, imag, i, width, keys[i])
            store_bins(scaled_ref, real, imag, i, width, times(taps, value))

    over_bins(step, shift_bins)

    @pl.loop(0, step // chunk)
    def _(index):
        start = pl.multiple_of(index * chunk, chunk)
        window = pl.ds(start, chunk)
        block = jnp.dot(
            inverse_ref[window, :], scaled_ref[...], preferred_element_type=jnp.float32
        )
        for i in range(count):
            rows = pl.ds(pl.multiple_of(i * step + start, chunk), chunk)
            shifted = block[:, lanes(i, width)]
            shifted_ref[rows, :] = shifted.astype(shifted_ref.dtype)
            product = shifted * values_ref[rows, :].astype(jnp.float32)
            source_ref[window, lanes(i, width)] = product.astype(source_ref.dtype)

    transform(table_ref, source_ref, spectrum_ref)
    for i in range(count):
        scaled_ref[:step, lanes(i, width)] = kernel_ref[pl.ds(i * step, step), :]
    transform(table_ref, scaled_ref.at[pl.ds(0, step), :], kernel_hat_ref)

    def state_bins(sign, real, imag):
        product = load_bins(spectrum_ref, real, imag, count, width)
        kernel = load_bins(kernel_hat_ref, real, imag, count, width)
        joined = with_last(product, sign)
        for m in range(count):
            store_bins(product_hat_ref, real, imag, m, width, product[m])
            total = None
            for d in range(m + 1):
                total = plus(total, times(kernel[d], joined[m - d]))
            store_bins(scaled_ref, real, imag, m, width, total)

    over_bins(step, state_bins)

    @pl.loop(0, step // chunk)
    def _(index):
        start = pl.multiple_of(index * chunk, chunk)
        window = pl.ds(start, chunk)
        block = jnp.dot(
            inverse_ref[window, :], scaled_ref[...], preferred_element_type=jnp.float32
        )
        for i in range(count):
            rows = pl.ds(pl.multiple_of(i * step + start, chunk), chunk)
            product = shifted_ref[rows, :].astype(jnp.float32) * values_ref[rows, :].astype(
                jnp.float32
            )
            state = block[:, lanes(i, width)] + skip_ref[...] * product
            state_ref[rows, :] = state.astype(state_ref.dtype)
            mixed_ref[rows, :] = (query_ref[rows, :].astype(jnp.float32) * state).astype(
                mixed_ref.dtype
            )


def mix_backward(
    count, step, width,
    table_ref, inverse_ref, grad_ref, query_ref, values_ref, shifted_ref, state_ref,
    keys_hat_ref, product_hat_ref, kernel_hat_ref, taps_hat_ref, skip_ref,
    grad_query_ref, grad_keys_ref, grad_values_ref, grad_kernel_ref, grad_taps_ref, grad_skip_ref,
    source_ref, spectrum_ref, scaled_ref, other_ref, taps_acc_ref,
):
    state_taps = grad_taps_ref.shape[0]
    chunk = min(step, 128)
    grad_skip_ref[...] = jnp.zeros_like(grad_skip_ref)

    @pl.loop(0, step // chunk)
    def _(index):
        start = pl.multiple_of(index * chunk, chunk)
        for i in range(count):
            rows = pl.ds(pl.multiple_of(i * step + start, chunk), chunk)
            grad = grad_ref[rows, :].astype(jnp.float32)
            grad_query_ref[rows, :] = (grad * state_ref[rows, :].astype(jnp.float32)).astype(
                grad_query_ref.dtype
            )
            grad_state = grad * query_ref[rows, :].astype(jnp.float32)
            product = shifted_ref[rows, :].astype(jnp.float32) * values_ref[rows, :].astype(
                jnp.float32
            )
            grad_skip_ref[...] += jnp.sum(grad_state * product, axis=0, keepdims=True)
            source_ref[pl.ds(start, chunk), lanes(i, width)] = grad_state.astype(source_ref.dtype)

    transform(table_ref, source_ref, spectrum_ref)

    def state_bins(sign, real, imag):
        joined = with_next(load_bins(spectrum_ref, real, imag, count, width), sign)
        kernel = load_bins(kernel_hat_ref, real, imag, count, width)
        for i in range(count):
            total = None
            for d in range(count - i):
                total = plus(total, times_conj(kernel[d], joined[i + d]))
            store_bins(scaled_ref, real, imag, i, width, total)
        product = load_bins(product_hat_ref, real, imag, count, width)
        for d in range(count):
            total = None
            for i in range(count - d):
                total = plus(total, times_conj(product[i], joined[i + d]))
            store_bins(other_ref, real, imag, d, width, total)

    over_bins(step, state_bins)

    @pl.loop(0, step // chunk)
    def _(index):
        start = pl.multiple_of(index * chunk, chunk)
        window = pl.ds(start, chunk)
        block = jnp.dot(
            inverse_ref[window, :], other_ref[...], preferred_element_type=jnp.float32
        )
        for i in range(count):
            rows = pl.ds(pl.multiple_of(i * step + start, chunk), chunk)
            grad_kernel_ref[rows, :] = block[:, lanes(i, width)]

    @pl.loop(0, step // chunk)
    def _(index):
        start = pl.multiple_of(index * chunk, chunk)
        window = pl.ds(start, chunk)
        block = jnp.dot(
            inverse_ref[window, :], scaled_ref[...], preferred_element_type=jnp.float32
        )
        for i in range(count):
            rows = pl.ds(pl.multiple_of(i * step + start, chunk), chunk)
            grad_state = grad_ref[rows, :].astype(jnp.float32) * query_ref[rows, :].astype(
                jnp.float32
            )
            grad_product = block[:, lanes(i, width)] + skip_ref[...] * grad_state
            grad_values_ref[rows, :] = (
                grad_product * shifted_ref[rows, :].astype(jnp.float32)
            ).astype(grad_values_ref.dtype)
            source_ref[window, lanes(i, width)] = (
                grad_product * values_ref[rows, :].astype(jnp.float32)
            ).astype(source_ref.dtype)

    transform(table_ref, source_ref, spectrum_ref)

    def shift_bins(sign, real, imag):
        joined = with_next(load_bins(spectrum_ref, real, imag, count, width), sign)
        keys = load_bins(keys_hat_ref, real, imag, count, width)
        taps = (taps_hat_ref[real, :], taps_hat_ref[imag, :])
        total = None
        for i in range(count):
            store_bins(scaled_ref, real, imag, i, width, times_conj(taps, joined[i]))
            total = plus(total, times_conj(keys[i], joined[i]))
        store_bins(taps_acc_ref, real, imag, 0, width, total)

    over_bins(step, shift_bins)
    grad_taps_ref[...] = jnp.dot(
        inverse_ref[:state_taps, :], taps_acc_ref[...], preferred_element_type=jnp.float32
    )

    @pl.loop(0, step // chunk)
    def _(index):
        start = pl.multiple_of(index * chunk, chunk)
        window = pl.ds(start, chunk)
        block = jnp.dot(
            inverse_ref[window, :], scaled_ref[...], preferred_element_type=jnp.float32
        )
        for i in range(count):
            rows = pl.ds(pl.multiple_of(i * step + start, chunk), chunk)
            grad_keys_ref[rows, :] = block[:, lanes(i, width)].astype(grad_keys_ref.dtype)


def mixer_sizes(channels):
    step = min(SLOT, 512)
    width = 128 if channels % 128 == 0 else channels
    return SLOT // step, step, width


def run_forward(query, keys, values, kernel, taps, skip):
    channels = keys.shape[1]
    count, step, width = mixer_sizes(channels)
    table = wave_table(step)
    forward_table = jnp.asarray(table, jnp.bfloat16)
    inverse_table = jnp.asarray(table.T / step, jnp.bfloat16)
    fixed = lambda shape: pl.BlockSpec(shape, lambda j: (0, 0), pipeline_mode=pl.Buffered(1))
    column = lambda rows: pl.BlockSpec((rows, width), lambda j: (0, j))
    wide = pl.BlockSpec((2 * step, count * width), lambda j: (0, j))
    shape = jax.ShapeDtypeStruct
    state_taps = taps.shape[0]
    return pl.pallas_call(
        functools.partial(mix_forward, count, step, width),
        grid=(channels // width,),
        in_specs=[fixed((2 * step, step)), fixed((step, 2 * step))]
        + [column(SLOT)] * 4
        + [column(state_taps), column(1)],
        out_specs=[column(SLOT)] * 3 + [wide] * 3 + [column(2 * step)],
        out_shape=[shape((SLOT, channels), jnp.bfloat16)] * 3
        + [shape((2 * step, count * channels), jnp.bfloat16)] * 3
        + [shape((2 * step, channels), jnp.float32)],
        scratch_shapes=[
            pltpu.VMEM((step, count * width), jnp.bfloat16),
            pltpu.VMEM((2 * step, count * width), jnp.float32),
            pltpu.VMEM((2 * step, count * width), jnp.bfloat16),
        ],
        compiler_params=pltpu.CompilerParams(vmem_limit_bytes=48 << 20),
        name="mix_forward",
    )(forward_table, inverse_table, query, keys, values, kernel, taps, skip)


def run_backward(grad, query, values, saved, skip, state_taps):
    channels = query.shape[1]
    count, step, width = mixer_sizes(channels)
    table = wave_table(step)
    forward_table = jnp.asarray(table, jnp.bfloat16)
    inverse_table = jnp.asarray(table.T / step, jnp.bfloat16)
    fixed = lambda shape: pl.BlockSpec(shape, lambda j: (0, 0), pipeline_mode=pl.Buffered(1))
    column = lambda rows: pl.BlockSpec((rows, width), lambda j: (0, j))
    wide = pl.BlockSpec((2 * step, count * width), lambda j: (0, j))
    shape = jax.ShapeDtypeStruct
    shifted, state, keys_hat, product_hat, kernel_hat, taps_hat = saved
    return pl.pallas_call(
        functools.partial(mix_backward, count, step, width),
        grid=(channels // width,),
        in_specs=[fixed((2 * step, step)), fixed((step, 2 * step))]
        + [column(SLOT)] * 5
        + [wide] * 3
        + [column(2 * step), column(1)],
        out_specs=[column(SLOT)] * 4 + [column(state_taps), column(1)],
        out_shape=[shape((SLOT, channels), jnp.bfloat16)] * 3
        + [
            shape((SLOT, channels), jnp.float32),
            shape((state_taps, channels), jnp.float32),
            shape((1, channels), jnp.float32),
        ],
        scratch_shapes=[
            pltpu.VMEM((step, count * width), jnp.bfloat16),
            pltpu.VMEM((2 * step, count * width), jnp.float32),
            pltpu.VMEM((2 * step, count * width), jnp.bfloat16),
            pltpu.VMEM((2 * step, count * width), jnp.bfloat16),
            pltpu.VMEM((2 * step, width), jnp.bfloat16),
        ],
        compiler_params=pltpu.CompilerParams(vmem_limit_bytes=48 << 20),
        name="mix_backward",
    )(
        forward_table, inverse_table, grad, query, values, shifted, state,
        keys_hat, product_hat, kernel_hat, taps_hat, skip,
    )


def powers(rate, turn, count, stride):
    places = (jnp.arange(count) * stride).astype(jnp.float32)
    fade = jnp.exp(-rate[:, :, None] * places)
    angle = turn[:, :, None] * places
    return fade * jnp.cos(angle), fade * jnp.sin(angle)


def mode_kernel(rate, turn, coef):
    coarse_re, coarse_im = powers(rate, turn, SLOT // FINE, FINE)
    fine_re, fine_im = powers(rate, turn, FINE, 1)
    first, second = coef[:, 0, :, None], coef[:, 1, :, None]
    left = jnp.concatenate(
        [first * coarse_re - second * coarse_im, -first * coarse_im - second * coarse_re], axis=1
    )
    right = jnp.concatenate([fine_re, fine_im], axis=1)
    kernel = jnp.einsum("cna,cnb->cab", left, right, precision=highest)
    return kernel.reshape(rate.shape[0], SLOT)


def mode_grads(rate, turn, coef, grad_kernel):
    modes = rate.shape[1]
    coarse_re, coarse_im = powers(rate, turn, SLOT // FINE, FINE)
    fine_re, fine_im = powers(rate, turn, FINE, 1)
    inner = jnp.arange(FINE).astype(jnp.float32)
    right = jnp.concatenate([fine_re, fine_im, inner * fine_re, inner * fine_im], axis=1)
    blocks = grad_kernel.reshape(rate.shape[0], SLOT // FINE, FINE)
    sums = jnp.einsum("cab,cnb->cna", blocks, right, precision=highest)
    low_re, low_im, slope_re, slope_im = (
        sums[:, i * modes : (i + 1) * modes] for i in range(4)
    )
    outer = (jnp.arange(SLOT // FINE) * FINE).astype(jnp.float32)
    slope_re, slope_im = outer * low_re + slope_re, outer * low_im + slope_im
    zero_re = jnp.sum(coarse_re * low_re - coarse_im * low_im, axis=2)
    zero_im = jnp.sum(coarse_re * low_im + coarse_im * low_re, axis=2)
    one_re = jnp.sum(coarse_re * slope_re - coarse_im * slope_im, axis=2)
    one_im = jnp.sum(coarse_re * slope_im + coarse_im * slope_re, axis=2)
    first, second = coef[:, 0], coef[:, 1]
    grad_coef = jnp.stack([zero_re, -zero_im], axis=1)
    grad_rate = -(first * one_re - second * one_im)
    grad_turn = -(first * one_im + second * one_re)
    return grad_rate, grad_turn, grad_coef


def two_parts(values):
    high = values.astype(jnp.bfloat16)
    return high, (values - high.astype(jnp.float32)).astype(jnp.bfloat16)


def local(
    tokens,
    cotangent,
    lengths,
    norm_gains,
    shift_taps,
    decay_rate,
    frequency,
    mode_coef,
    skip_gain,
    qkv_weight,
    out_weight,
    up_weight,
    down_weight,
):
    parts = lax.axis_size("seq")
    slots, length, width = tokens.shape
    half = parts // slots
    place = lax.axis_index("seq")
    slot, rank = place // half, place % half
    channels = width // half
    state_taps = shift_taps.shape[1]
    gather = functools.partial(lax.all_gather, axis_name=both, axis=0, tiled=True)
    scatter = functools.partial(
        lax.psum_scatter, axis_name=both, scatter_dimension=0, tiled=True
    )

    def swap(values):
        return lax.ppermute(values, "seq", [(i, (i + half) % parts) for i in range(parts)])

    def pick(pair, index):
        return lax.dynamic_index_in_dim(pair, index, 0, keepdims=False)

    def rows_of(pair):
        kept, came = pick(pair, slot), swap(pick(pair, 1 - slot))
        low = jnp.where(slot == 0, kept, came)
        high = jnp.where(slot == 0, came, kept)
        return jnp.concatenate([low, high], axis=0)

    def home_of(rows, dtype):
        pair = rows.reshape(2, length, width)
        kept = pick(pair, slot).astype(dtype)
        came = swap(pick(pair, 1 - slot).astype(jnp.bfloat16)).astype(dtype)
        return jnp.stack(
            [jnp.where(slot == 0, kept, came), jnp.where(slot == 0, came, kept)], axis=0
        )

    token_rows = rows_of(tokens)
    cot_rows = rows_of(cotangent)
    qkv_full = gather(qkv_weight)
    gain_high, gain_low = two_parts(norm_gains)
    skip_high, skip_low = two_parts(skip_gain[:, None])
    kernel_own = mode_kernel(decay_rate, frequency, mode_coef)
    small = jnp.concatenate(
        [
            kernel_own.astype(jnp.bfloat16),
            shift_taps.astype(jnp.bfloat16),
            gain_high,
            gain_low,
            skip_high,
            skip_low,
            jnp.zeros((kernel_own.shape[0], 58), jnp.bfloat16),
        ],
        axis=1,
    )
    small_full = gather(small)
    out_full = gather(out_weight)
    up_full = gather(up_weight)
    down_full = gather(down_weight)
    base = SLOT + state_taps
    extra = small_full[:, base : base + 6].astype(jnp.float32)
    gain_one, gain_two = extra[:, 0] + extra[:, 2], extra[:, 1] + extra[:, 3]
    start = rank * channels
    mine = lax.dynamic_slice_in_dim(small_full, start, channels, 0)
    kernel_mine = mine[:, :SLOT].T
    taps_mine = mine[:, SLOT:base].T
    skip_mine = lax.dynamic_slice_in_dim(extra[:, 4] + extra[:, 5], start, channels, 0)[None, :]

    input_rows = token_rows.astype(jnp.float32)
    normed_one, norm_one_back = jax.vjp(layer_norm, input_rows, gain_one)
    normed_low = normed_one.astype(jnp.bfloat16)
    projected = mat_dot(normed_low, qkv_full, ((1,), (0,))).astype(jnp.bfloat16)

    def shift_rank(values, k):
        pairs = [(i, i // half * half + (i % half + k) % half) for i in range(parts)]
        return lax.ppermute(values, "seq", pairs)

    def to_channels(values, fold):
        rows = values.shape[0]
        by_rank = values.reshape(rows, fold, half, channels)
        pieces = []
        for k in range(half):
            piece = lax.dynamic_index_in_dim(by_rank, (rank + k) % half, 2, keepdims=False)
            pieces.append(piece if k == 0 else shift_rank(piece, k))
        ordered = jnp.stack(
            [
                lax.select_n((rank - i) % half, *pieces) if half > 1 else pieces[0]
                for i in range(half)
            ],
            axis=0,
        )
        ordered = ordered.reshape(half, 2, length, fold, channels)
        return ordered.transpose(1, 0, 2, 3, 4).reshape(SLOT, fold, channels)

    def to_rows(values, fold):
        by_rank = values.reshape(2, half, length, fold, channels)
        pieces = []
        for k in range(half):
            piece = lax.dynamic_index_in_dim(by_rank, (rank + k) % half, 1, keepdims=False)
            piece = piece.reshape(2 * length, fold, channels)
            pieces.append(piece if k == 0 else shift_rank(piece, k))
        ordered = [
            lax.select_n((rank - i) % half, *pieces) if half > 1 else pieces[0]
            for i in range(half)
        ]
        return jnp.concatenate(ordered, axis=2).reshape(2 * length, fold * width)

    triple = to_channels(projected, 3)
    query, keys, values = triple[:, 0], triple[:, 1], triple[:, 2]
    mixed, *saved = run_forward(query, keys, values, kernel_mine, taps_mine, skip_mine)
    mixed_rows = to_rows(mixed, 1)
    hidden = input_rows + mat_dot(mixed_rows, out_full, ((1,), (0,)))
    normed_two, norm_two_back = jax.vjp(layer_norm, hidden, gain_two)
    normed_two_low = normed_two.astype(jnp.bfloat16)
    pre_act = mat_dot(normed_two_low, up_full, ((1,), (0,)))
    activity, gelu_back = jax.vjp(exact_gelu, pre_act)
    activity_low = activity.astype(jnp.bfloat16)
    reach = lax.dynamic_index_in_dim(
        lengths, lax.axis_index("dp") * slots + slot, 0, keepdims=False
    )
    ids = rank * length + jnp.arange(length, dtype=jnp.int32)
    ids = jnp.concatenate([ids, ids + SLOT // 2])
    live_mask = (ids < reach).astype(jnp.float32)[:, None]
    result_rows = live_mask * (hidden + mat_dot(activity_low, down_full, ((1,), (0,))))
    layer_out = home_of(result_rows, jnp.bfloat16)

    grad_sum = live_mask * cot_rows.astype(jnp.float32)
    grad_branch = grad_sum.astype(jnp.bfloat16)
    down_grad = mat_dot(activity_low, grad_branch, ((0,), (0,)))
    grad_act = mat_dot(grad_branch, down_full, ((1,), (1,)))
    grad_pre = gelu_back(grad_act)[0].astype(jnp.bfloat16)
    up_grad = mat_dot(normed_two_low, grad_pre, ((0,), (0,)))
    grad_normed = mat_dot(grad_pre, up_full, ((1,), (1,)))
    grad_hidden_norm, grad_gain_two = norm_two_back(grad_normed)
    grad_hidden = grad_sum + grad_hidden_norm
    up_share = scatter(up_grad)
    down_share = scatter(down_grad)
    grad_mix = grad_hidden.astype(jnp.bfloat16)
    out_grad = mat_dot(mixed_rows, grad_mix, ((0,), (0,)))
    grad_mixed = mat_dot(grad_mix, out_full, ((1,), (1,))).astype(jnp.bfloat16)
    channel_grad = to_channels(grad_mixed, 1)[:, 0]
    grad_query, grad_keys, grad_values, grad_kernel, grad_taps, grad_skip = run_backward(
        channel_grad, query, values, saved, skip_mine, state_taps
    )
    grad_projected = to_rows(jnp.stack([grad_query, grad_keys, grad_values], axis=1), 3)
    qkv_grad = mat_dot(normed_low, grad_projected, ((0,), (0,)))
    grad_normed_one = mat_dot(grad_projected, qkv_full, ((1,), (1,)))
    grad_input_norm, grad_gain_one = norm_one_back(grad_normed_one)
    input_grad = home_of(grad_hidden + grad_input_norm, jnp.float32)

    packed = jnp.concatenate([grad_kernel, grad_taps, grad_skip], axis=0).T
    wide = lax.dynamic_update_slice_in_dim(
        jnp.zeros((width, packed.shape[1]), jnp.float32), packed, start, 0
    )
    wide = jnp.concatenate([wide, grad_gain_one[:, None], grad_gain_two[:, None]], axis=1)
    wide = jnp.pad(wide, ((0, 0), (0, -wide.shape[1] % 128)))
    qkv_share, out_share, small_share = scatter(qkv_grad), scatter(out_grad), scatter(wide)
    grad_rate, grad_turn, grad_coef = mode_grads(
        decay_rate, frequency, mode_coef, small_share[:, :SLOT]
    )
    return (
        layer_out,
        input_grad,
        small_share[:, base + 1 : base + 3],
        small_share[:, SLOT:base],
        grad_rate,
        grad_turn,
        grad_coef,
        small_share[:, base],
        qkv_share,
        out_share,
        up_share,
        down_share,
    )


def solution(mesh):
    return jax.shard_map(
        local,
        mesh=mesh,
        in_specs=(
            P("dp", "seq", None),
            P("dp", "seq", None),
            P(),
            P(("dp", "seq"), None),
            P(("dp", "seq"), None),
            P(("dp", "seq"), None),
            P(("dp", "seq"), None),
            P(("dp", "seq"), None, None),
            P(("dp", "seq")),
            P(("dp", "seq"), None),
            P(("dp", "seq"), None),
            P(("dp", "seq"), None),
            P(("dp", "seq"), None),
        ),
        out_specs=(
            P("dp", "seq", None),
            P("dp", "seq", None),
            P(("dp", "seq"), None),
            P(("dp", "seq"), None),
            P(("dp", "seq"), None),
            P(("dp", "seq"), None),
            P(("dp", "seq"), None, None),
            P(("dp", "seq")),
            P(("dp", "seq"), None),
            P(("dp", "seq"), None),
            P(("dp", "seq"), None),
            P(("dp", "seq"), None),
        ),
        check_vma=False,
    )
```

time: 4140 us -> 1140 us (0.28)
  matrix products: 1480 us -> 134 us
  other arithmetic: 695 us -> 49.1 us
  local copies, waits for them, and re-layouts: 707 us -> 86.4 us
  blocking collectives: 357 us -> 0 us
  loops' own time: 75.8 us -> 0 us
  Pallas kernels: 0 us -> 63.4 us
    dot_general x2592 -> x2, matrix products: 1390 us -> 3.47 us  [the longest x1 2.58 us: mode_grads(): sums = jnp.einsum('cab,cnb->cna', blocks, right, precision=highest)]
    reduce_sum x74 -> x1, other arithmetic: 470 us -> 2.12 us  [mode_grads(): zero_re = jnp.sum(coarse_re * low_re - coarse_im * low_im, axis=2)]
    all_gather x5 -> x0, blocking collectives: 216 us -> none  [the longest x1 56.9 us: local(): lax.all_gather(norm_gains, ('dp', 'seq'), axis=0, tiled=True)]
    reshape x402 -> x2, local copies, waits for them, and re-layouts: 197 us -> 10 us  [the longest x1 9.89 us: to_channels(): by_rank = values.reshape(rows, fold, half, channels)]
    squeeze x264 -> x3, local copies, waits for them, and re-layouts: 172 us -> 3.34 us  [the longest x1 2.34 us: local(): query, keys, values = (triple[:, 0], triple[:, 1], triple[:, 2])]
    all_gather x4 -> x5, waiting for transfers between devices: 0.06 us -> 156 us  [the longest x1 60 us: local(): qkv_full = gather(qkv_weight)]
    unnamed x2 -> x0, blocking collectives: 118 us -> none
    div x193 -> x0, local copies, waits for them, and re-layouts: 116 us -> none  [the longest x192 116 us: inverse_dft(): joined = joined / float(first_size * second_size)]
where the time goes in v1:
time: 1140 us
  waiting for transfers between devices  782 us (69%)
  matrix products  134 us (12%)
  local copies, waits for them, and re-layouts  86.4 us (8%)
  Pallas kernels  63.4 us (6%)
  other arithmetic  49.1 us (4%)
  between operations  15.5 us (1%)
    reduce_scatter x1, waiting for transfers between devices, local(): down_share = scatter(down_grad)  142 us
    reduce_scatter x1, waiting for transfers between devices, local(): up_share = scatter(up_grad)  142 us
    dot_general x12, matrix products, mat_dot(): lax.dot_general(left, right, (contract, ((), ())), preferred_element_type...  131 us
    reduce_scatter x1, waiting for transfers between devices, local(): scatter(qkv_grad)  124 us
    reduce_scatter x1, waiting for transfers between devices, local(): scatter(out_grad)  93.6 us
    unnamed x11, waiting for transfers between devices  73.3 us
    all_gather x1, waiting for transfers between devices, local(): qkv_full = gather(qkv_weight)  60 us
    ppermute x4, waiting for transfers between devices, swap(): lax.ppermute(values, 'seq', [(i, (i + half) % parts) for i in range(parts)])  49.6 us
  transfers between devices with their start and end apart: 18, of which 13 were waited for; matrix products, arithmetic and copies ran while one was open for 16% of the time, Pallas kernels for 3%

profile of v1, /device:TPU:0, one launch (start us, length us, event | category | flops | bytes accessed | tf_op | source)
XLA Modules:
  0.0 1138.8 jit_solution(12096042549524817088)
XLA Ops:
  22.3 18.3 %collective-permute-done = bf16[512,768]{1,0:T(8,128)(2,1)S(1)} collective-permute-done((bf16[512,768]{1,0:T(8,128)(2,1)S(1)}, bf16[512,768]{1,0:T(8,128)(2,1)S(1)}, u32[]{:S(2)}, u32[]{:S(2)}) %collective-permute-start) | collective-permute-done | bytes 786464 | tf_op jit(solution)/shard_map/ppermute | solution.py:439
  42.8 36.5 %all-gather.6.cloned.1.call-done = bf16[768,2176]{1,0:T(8,128)(2,1)} async-done(((bf16[24,2176]{1,0:T(8,128)(2,1)}), bf16[768,2176]{1,0:T(8,128)(2,1)}) %all-gather.6.cloned.1.call-update) | async-done | bytes 3342352 | tf_op jit(solution)/shard_map/all_gather | solution.py:476
  81.1 60.0 %all-gather.8.cloned.1.call-done = bf16[768,2304]{1,0:T(8,128)(2,1)} async-done(((bf16[24,2304]{1,0:T(8,128)(2,1)}), bf16[768,2304]{1,0:T(8,128)(2,1)}) %all-gather.8.cloned.1.call-update) | async-done | bytes 3538960 | tf_op jit(solution)/shard_map/all_gather | solution.py:460
  141.1 8.6 convolution_convert_fusion
  149.7 9.9 reshape.215
  159.6 12.1 %constant_dynamic-slice_fusion.8 = (bf16[1024,3,1,384]{3,2,1,0:T(2,128)(2,1)}, bf16[1024,3,1,384]{3,2,1,0:T(2,128)(2,1)S(1)}) fusion(bf16[1024,3,2,384]{3,2,1,0:T(2,128)(2,1)} %reshape.215, s32[]{:T(128)S(6)} %select_n.190, s32[]{:T(128)S(6)} %select_n.192), kind=kLoop, calls=%fused_computation.142 | loop fusion | bytes 9437192 | tf_op jit(solution)/shard_map/jit(dynamic_index_in_dim)/dynamic_slice | solution.py:503
  180.5 3.8 broadcast_select_fusion.1
  187.5 29.5 %mix_forward.1 = (bf16[2048,384]{1,0:T(8,128)(2,1)S(1)}, bf16[2048,384]{1,0:T(8,128)(2,1)S(1)}, bf16[2048,384]{1,0:T(8,128)(2,1)}, bf16[1024,1536]{1,0:T(8,128)(...) custom-call(bf16[1024,512]{1,0:T(8,128)(2,1)S(1)} %copy-done, ...), custom_call_target="tpu_custom_call" | custom-call | tf_op jit(solution)/shard_map/mix_forward/pallas_call | solution.py:303
  225.9 3.5 fusion.65
  231.7 32.1 %all-gather.12.cloned.1.call-done = bf16[768,3072]{1,0:T(8,128)(2,1)} async-done(((bf16[24,3072]{1,0:T(8,128)(2,1)}), bf16[768,3072]{1,0:T(8,128)(2,1)}) %all-gather.12.cloned.1.call-update) | async-done | bytes 4718608 | tf_op jit(solution)/shard_map/all_gather | solution.py:478
  263.8 38.0 %multiply_convert_fusion = (bf16[1024,3072]{1,0:T(8,128)(2,1)}, f32[1024,3072]{1,0:T(8,128)}, f32[1024,3072]{1,0:T(8,128)}) fusion(bf16[768,3072]{1,0:T(8,128)(2,1)} %all-gather.12.cloned.1.call-done, f32[1024,768]{1,0:T(8,128)} %copy-done.3, f32[768]{0:T(1024)S(1)} %get-tuple-element.132, f32[1024]{0:T(1024)S(1)} %fusion.50, ...), kind=kOutput, calls=%fused_computation.3 | convolution fusion | flops 5039456256 | bytes 39332864 | tf_op jit(solution)/shard_map/dot_general | solution.py:28
  301.7 27.2 %all-gather.14.cloned.1.call-done = bf16[3072,768]{1,0:T(8,128)(2,1)} async-done(((bf16[96,768]{1,0:T(8,128)(2,1)}), bf16[3072,768]{1,0:T(8,128)(2,1)}) %all-gather.14.cloned.1.call-update) | async-done | bytes 4718608 | tf_op jit(solution)/shard_map/all_gather | solution.py:479
  329.0 16.2 %add_convert_fusion = bf16[1024,3072]{1,0:T(8,128)(2,1)} fusion(f32[1024,3072]{1,0:T(8,128)} %get-tuple-element.99, f32[1024,3072]{1,0:T(8,128)} %get-tuple-element.147, bf16[3072,768]{1,0:T(8,128)(2,1)} %all-gather.14.cloned.1.call-done, f32[1024]{0:T(1024)S(1)} %fusion.48, bf16[512,768]{1,0:T(8,128)(2,1)} %get-tuple-element.116, ...), kind=kOutput, calls=%fused_computation.2 | convolution fusion | flops 4880596992 | bytes 37752832 | tf_op jit(solution)/shard_map/dot_general | solution.py:28
  345.1 9.8 multiply_reduce_fusion
  368.9 33.9 %mix_backward.1 = (bf16[2048,384]{1,0:T(8,128)(2,1)S(1)}, bf16[2048,384]{1,0:T(8,128)(2,1)S(1)}, bf16[2048,384]{1,0:T(8,128)(2,1)}, f32[2048,384]{1,0:T(8,128)},...) custom-call(bf16[1024,512]{1,0:T(8,128)(2,1)S(1)} %copy-done, bf16[512,1024]{1,0:T(8,128)(2,1)S(1)} %copy-done.1, ...), custom_call_target="tpu_custom_call" | custom-call | tf_op jit(solution)/shard_map/mix_backward/pallas_call | solution.py:334
  413.7 3.3 broadcast_in_dim.24
  424.5 6.8 copy.90
  431.3 8.2 fusion.15
  442.4 8.3 concatenate.49
  450.7 6.1 pad.4
  456.8 5.0 fusion.28
  462.0 10.7 fusion.59
  472.7 10.2 fusion.55
  483.3 10.1 fusion.35
  493.4 8.8 add_multiply_fusion
  509.1 16.3 %collective-permute-done.3 = bf16[512,768]{1,0:T(8,128)(2,1)} collective-permute-done((bf16[512,768]{1,0:T(8,128)(2,1)}, bf16[512,768]{1,0:T(8,128)(2,1)}, u32[]{:S(2)}, u32[]{:S(2)}) %collective-permute-start.3) | collective-permute-done | bytes 786464 | tf_op jit(solution)/shard_map/ppermute | solution.py:439
  528.1 15.1 %collective-permute-done.7 = bf16[512,768]{1,0:T(8,128)(2,1)} collective-permute-done((bf16[512,768]{1,0:T(8,128)(2,1)}, bf16[512,768]{1,0:T(8,128)(2,1)}, u32[]{:S(2)}, u32[]{:S(2)}) %collective-permute-start.7) | collective-permute-done | bytes 786464 | tf_op jit(solution)/shard_map/ppermute | solution.py:439
  546.5 71.3 %all-reduce.4.cloned.1.call-done = f32[768,2176]{1,0:T(8,128)} async-done(((f32[768,2176]{1,0:T(8,128)}), f32[768,2176]{1,0:T(8,128)}) %all-reduce.4.cloned.1.call-update) | async-done | bytes 6684688
  629.2 93.6 %reduce-scatter.7.cloned.1.call-done = f32[24,768]{1,0:T(8,128)} async-done(((f32[768,768]{1,0:T(8,128)}), f32[24,768]{1,0:T(8,128)}) %reduce-scatter.7.cloned.1.call-update) | async-done | bytes 73744 | tf_op jit(solution)/shard_map/reduce_scatter | solution.py:577
  722.8 142.1 %reduce-scatter.9.cloned.1.call-done = f32[24,3072]{1,0:T(8,128)} async-done(((f32[768,3072]{1,0:T(8,128)}), f32[24,3072]{1,0:T(8,128)}) %reduce-scatter.9.cloned.1.call-update) | async-done | bytes 294928 | tf_op jit(solution)/shard_map/reduce_scatter | solution.py:556
  865.0 124.4 %reduce-scatter.5.cloned.1.call-done = f32[24,2304]{1,0:T(8,128)} async-done(((f32[768,2304]{1,0:T(8,128)}), f32[24,2304]{1,0:T(8,128)}) %reduce-scatter.5.cloned.1.call-update) | async-done | bytes 221200 | tf_op jit(solution)/shard_map/reduce_scatter | solution.py:577
  989.3 142.2 %reduce-scatter.11.cloned.1.call-done = f32[96,768]{1,0:T(8,128)} async-done(((f32[3072,768]{1,0:T(8,128)}), f32[96,768]{1,0:T(8,128)}) %reduce-scatter.11.cloned.1.call-update) | async-done | bytes 294928 | tf_op jit(solution)/shard_map/reduce_scatter | solution.py:557
  (231 shorter events, 101.5 us)
Async XLA Ops:
  7.2 72.0 %all-gather.6.cloned.1.call-start = ((), (), s32[]{:S(2)}) async-start(), calls=%async_computation.4 | async-start | bytes 3446784 | tf_op jit(solution)/shard_map/all_gather | solution.py:476
  16.9 124.3 %all-gather.8.cloned.1.call-start = ((), (), s32[]{:S(2)}) async-start(), calls=%async_computation.5 | async-start | bytes 3649536 | tf_op jit(solution)/shard_map/all_gather | solution.py:460
  17.6 208.3 %all-gather.10.cloned.1.call-start = ((), (), s32[]{:S(2)}) async-start(), calls=%async_computation.6 | async-start | bytes 1216512 | tf_op jit(solution)/shard_map/all_gather | solution.py:477
  18.3 245.4 %all-gather.12.cloned.1.call-start = ((), (), s32[]{:S(2)}) async-start(), calls=%async_computation.7 | async-start | bytes 4866048 | tf_op jit(solution)/shard_map/all_gather | solution.py:478
  18.9 310.0 %all-gather.14.cloned.1.call-start = ((), (), s32[]{:S(2)}) async-start(), calls=%async_computation.8 | async-start | bytes 4866048 | tf_op jit(solution)/shard_map/all_gather | solution.py:479
  19.3 21.3 %collective-permute-start = (bf16[512,768]{1,0:T(8,128)(2,1)S(1)}, bf16[512,768]{1,0:T(8,128)(2,1)S(1)}, u32[]{:S(2)}, u32[]{:S(2)}) collective-permute-start(bf16[512,768]{1,0:T(8,128)(2,1)S(1)} %dynamic-slice_bitcast_fusion.1), channel_id=1, source_target_pairs={{0,2},{1,3},{2,0},{3,1},{4,6},{5,7},{6,4},{7,5},{8,10},{9,11},{10,... | collective-permute-start | bytes 2359304 | tf_op jit(solution)/shard_map/ppermute | solution.py:439
  41.8 99.3 %copy-start.11 = (bf16[512,768]{1,0:T(8,128)(2,1)}, bf16[512,768]{1,0:T(8,128)(2,1)S(1)}, u32[]{:S(2)}) copy-start(bf16[512,768]{1,0:T(8,128)(2,1)S(1)} %get-tuple-element.120) | copy-start | bytes 2359300
  41.8 184.1 %copy-start.8 = (bf16[512,768]{1,0:T(8,128)(2,1)}, bf16[512,768]{1,0:T(8,128)(2,1)S(1)}, u32[]{:S(2)}) copy-start(bf16[512,768]{1,0:T(8,128)(2,1)S(1)} %get-tuple-element.119) | copy-start | bytes 2359300
  42.1 107.6 %copy-start.41 = (f32[1024]{0:T(1024)}, f32[1024]{0:T(1024)S(1)}, u32[]{:S(2)}) copy-start(f32[1024]{0:T(1024)S(1)} %broadcast_multiply_fusion.3) | copy-start | bytes 12292
  42.8 107.0 %copy-start.45 = (f32[1024]{0:T(1024)}, f32[1024]{0:T(1024)S(1)}, u32[]{:S(2)}) copy-start(f32[1024]{0:T(1024)S(1)} %fusion.49) | copy-start | bytes 12292
  81.1 68.6 %copy-start.43 = (f32[768]{0:T(1024)}, f32[768]{0:T(1024)S(1)}, u32[]{:S(2)}) copy-start(f32[768]{0:T(1024)S(1)} %get-tuple-element.131) | copy-start | bytes 9220
  173.5 7.0 collective-permute-start.1
  174.7 46.0 %collective-permute-start.4 = (bf16[512,768]{1,0:T(8,128)(2,1)}, bf16[512,768]{1,0:T(8,128)(2,1)}, u32[]{:S(2)}, u32[]{:S(2)}) collective-permute-start(bf16[512,768]{1,0:T(8,128)(2,1)} %dynamic-slice_bitcast_fusion), channel_id=1, source_target_pairs={{0,2},{1,3},{2,0},{3,1},{4,6},{5,7},{6,4},{7,5},{8,10},{9,11},{10,... | collective-permute-start | bytes 2359304 | tf_op jit(solution)/shard_map/ppermute | solution.py:439
  219.4 4.0 collective-permute-start.2
  219.5 398.4 %all-reduce.4.cloned.1.call-start = ((), (), s32[]{:S(2)}) async-start(), calls=%async_computation.13 | async-start | bytes 13369344
  363.4 2.6 collective-permute-start.5
  407.4 11.6 %collective-permute-start.6 = (bf16[1024,3,384]{2,0,1:T(8,128)(2,1)}, bf16[1024,3,384]{2,0,1:T(8,128)(2,1)}, u32[]{:S(2)}, u32[]{:S(2)}) collective-permute-start(bf16[1024,3,384]{2,0,1:T(8,128)(2,1)} %bitcast.45), channel_id=1, source_target_pairs={{0,1},{1,0},{2,3},{3,2},{4,5},{5,4},{6,7},{7,6},{8,9},{9,8},{10,11... | collective-permute-start | bytes 7077896 | tf_op jit(solution)/shard_map/ppermute | solution.py:496
  456.8 266.1 %reduce-scatter.7.cloned.1.call-start = ((), (), s32[]{:S(2)}) async-start(), calls=%async_computation.10 | async-start | bytes 2433024 | tf_op jit(solution)/shard_map/reduce_scatter | solution.py:577
  461.9 403.1 %reduce-scatter.9.cloned.1.call-start = ((), (), s32[]{:S(2)}) async-start(), calls=%async_computation.11 | async-start | bytes 9732096 | tf_op jit(solution)/shard_map/reduce_scatter | solution.py:556
  472.7 516.6 %reduce-scatter.5.cloned.1.call-start = ((), (), s32[]{:S(2)}) async-start(), calls=%async_computation.9 | async-start | bytes 7299072 | tf_op jit(solution)/shard_map/reduce_scatter | solution.py:577
  483.0 648.5 %reduce-scatter.11.cloned.1.call-start = ((), (), s32[]{:S(2)}) async-start(), calls=%async_computation.12 | async-start | bytes 9732096 | tf_op jit(solution)/shard_map/reduce_scatter | solution.py:557
  503.3 22.1 %collective-permute-start.3 = (bf16[512,768]{1,0:T(8,128)(2,1)}, bf16[512,768]{1,0:T(8,128)(2,1)}, u32[]{:S(2)}, u32[]{:S(2)}) collective-permute-start(bf16[512,768]{1,0:T(8,128)(2,1)} %fusion.30), channel_id=1, source_target_pairs={{0,2},{1,3},{2,0},{3,1},{4,6},{5,7},{6,4},{7,5},{8,10},{9,11},{10,... | collective-permute-start | bytes 2359304 | tf_op jit(solution)/shard_map/ppermute | solution.py:439
  508.5 34.7 %collective-permute-start.7 = (bf16[512,768]{1,0:T(8,128)(2,1)}, bf16[512,768]{1,0:T(8,128)(2,1)}, u32[]{:S(2)}, u32[]{:S(2)}) collective-permute-start(bf16[512,768]{1,0:T(8,128)(2,1)} %fusion.31), channel_id=1, source_target_pairs={{0,2},{1,3},{2,0},{3,1},{4,6},{5,7},{6,4},{7,5},{8,10},{9,11},{10,... | collective-permute-start | bytes 2359304 | tf_op jit(solution)/shard_map/ppermute | solution.py:439
  544.6 74.4 %copy-start.25 = (f32[24,32,64]{2,1,0:T(8,128)S(1)}, f32[24,32,64]{2,1,0:T(8,128)}, u32[]{:S(2)}) copy-start(f32[24,32,64]{2,1,0:T(8,128)} %copy-done.24) | copy-start | bytes 589828
  544.6 74.4 %copy-start.27 = (f32[24,32,64]{2,1,0:T(8,128)S(1)}, f32[24,32,64]{2,1,0:T(8,128)}, u32[]{:S(2)}) copy-start(f32[24,32,64]{2,1,0:T(8,128)} %copy-done.26) | copy-start | bytes 589828
  544.6 74.4 %copy-start.32 = (f32[24,32,64]{2,1,0:T(8,128)S(1)}, f32[24,32,64]{2,1,0:T(8,128)}, u32[]{:S(2)}) copy-start(f32[24,32,64]{2,1,0:T(8,128)} %get-tuple-element.137) | copy-start | bytes 589828
  544.6 74.4 %copy-start.33 = (f32[24,32,64]{2,1,0:T(8,128)S(1)}, f32[24,32,64]{2,1,0:T(8,128)}, u32[]{:S(2)}) copy-start(f32[24,32,64]{2,1,0:T(8,128)} %get-tuple-element.139) | copy-start | bytes 589828
  546.5 75.1 %copy-start.35 = (f32[24,32]{1,0:T(8,128)S(1)}, f32[24,32]{1,0:T(8,128)}, u32[]{:S(2)}) copy-start(f32[24,32]{1,0:T(8,128)} %copy-done.34) | copy-start | bytes 9220
  546.5 75.1 %copy-start.38 = (f32[24,32]{1,0:T(8,128)S(1)}, f32[24,32]{1,0:T(8,128)}, u32[]{:S(2)}) copy-start(f32[24,32]{1,0:T(8,128)} %param.23) | copy-start | bytes 9220
  546.5 75.1 %copy-start.51 = (f32[32]{0:T(128)S(1)}, f32[32]{0:T(128)}, u32[]{:S(2)}) copy-start(f32[32]{0:T(128)} %copy-done.50) | copy-start | bytes 388
  546.5 82.1 %copy-start.37 = (f32[24,1,32]{2,1,0:T(1,128)S(1)}, f32[24,1,32]{2,1,0:T(1,128)}, u32[]{:S(2)}) copy-start(f32[24,1,32]{2,1,0:T(1,128)} %copy-done.36) | copy-start | bytes 9220
  546.5 82.1 %copy-start.40 = (f32[24,1,32]{2,1,0:T(1,128)S(1)}, f32[24,1,32]{2,1,0:T(1,128)}, u32[]{:S(2)}) copy-start(f32[24,1,32]{2,1,0:T(1,128)} %copy-done.39) | copy-start | bytes 9220
  (42 other events, 335.8 us)
Sparse Core Ops, SparseCore 0:
  17.0 62.2 all-gather.5
  82.2 58.9 all-gather.7
  144.1 54.1 all-gather.9
  201.0 62.6 all-gather.11
  266.5 62.4 all-gather.13
  456.9 160.9 all-reduce.3
  623.7 99.0 reduce-scatter.6
  730.3 134.6 reduce-scatter.8
  871.2 118.0 reduce-scatter.4
  996.7 134.8 reduce-scatter.10

commit v2 on v1

--- a/solution.py
+++ b/solution.py
@@ -104,17 +104,20 @@
 
 def mix_forward(
     count, step, width,
-    table_ref, inverse_ref, query_ref, keys_ref, values_ref, kernel_ref, taps_ref, skip_ref,
+    table_ref, inverse_ref, table_low_ref, query_ref, keys_ref, values_ref, kernel_ref, taps_ref, skip_ref,
     mixed_ref, shifted_ref, state_ref, keys_hat_ref, product_hat_ref, kernel_hat_ref, taps_hat_ref,
-    source_ref, spectrum_ref, scaled_ref,
+    source_ref, spectrum_ref, scaled_ref, product_ref,
 ):
-    state_taps = taps_ref.shape[0]
+    state_taps = taps_ref.shape[0] // 2
     chunk = min(step, 128)
     for i in range(count):
         source_ref[:, lanes(i, width)] = keys_ref[pl.ds(i * step, step), :]
     transform(table_ref, source_ref, spectrum_ref)
-    taps_hat_ref[...] = jnp.dot(
-        table_ref[:, :state_taps], taps_ref[...], preferred_element_type=jnp.float32
+    narrow = table_ref[:, :state_taps]
+    taps_hat_ref[...] = (
+        jnp.dot(narrow, taps_ref[:state_taps, :], preferred_element_type=jnp.float32)
+        + jnp.dot(narrow, taps_ref[state_taps:, :], preferred_element_type=jnp.float32)
+        + jnp.dot(table_low_ref[...], taps_ref[:state_taps, :], preferred_element_type=jnp.float32)
     )
 
     def shift_bins(sign, real, imag):
@@ -138,6 +141,7 @@
             shifted = block[:, lanes(i, width)]
             shifted_ref[rows, :] = shifted.astype(shifted_ref.dtype)
             product = shifted * values_ref[rows, :].astype(jnp.float32)
+            product_ref[rows, :] = product
             source_ref[window, lanes(i, width)] = product.astype(source_ref.dtype)
 
     transform(table_ref, source_ref, spectrum_ref)
@@ -167,10 +171,7 @@
         )
         for i in range(count):
             rows = pl.ds(pl.multiple_of(i * step + start, chunk), chunk)
-            product = shifted_ref[rows, :].astype(jnp.float32) * values_ref[rows, :].astype(
-                jnp.float32
-            )
-            state = block[:, lanes(i, width)] + skip_ref[...] * product
+            state = block[:, lanes(i, width)] + skip_ref[...] * product_ref[rows, :]
             state_ref[rows, :] = state.astype(state_ref.dtype)
             mixed_ref[rows, :] = (query_ref[rows, :].astype(jnp.float32) * state).astype(
                 mixed_ref.dtype
@@ -289,23 +290,28 @@
     return SLOT // step, step, width
 
 
+def mixer_tables(step):
+    table = wave_table(step)
+    high = table.astype(jnp.bfloat16)
+    low = (table - high.astype(np.float64)).astype(jnp.bfloat16)
+    return jnp.asarray(high), jnp.asarray(table.T / step, jnp.bfloat16), jnp.asarray(low)
+
+
 def run_forward(query, keys, values, kernel, taps, skip):
     channels = keys.shape[1]
     count, step, width = mixer_sizes(channels)
-    table = wave_table(step)
-    forward_table = jnp.asarray(table, jnp.bfloat16)
-    inverse_table = jnp.asarray(table.T / step, jnp.bfloat16)
+    forward_table, inverse_table, low_table = mixer_tables(step)
     fixed = lambda shape: pl.BlockSpec(shape, lambda j: (0, 0), pipeline_mode=pl.Buffered(1))
     column = lambda rows: pl.BlockSpec((rows, width), lambda j: (0, j))
     wide = pl.BlockSpec((2 * step, count * width), lambda j: (0, j))
     shape = jax.ShapeDtypeStruct
-    state_taps = taps.shape[0]
+    state_taps = taps.shape[0] // 2
     return pl.pallas_call(
         functools.partial(mix_forward, count, step, width),
         grid=(channels // width,),
-        in_specs=[fixed((2 * step, step)), fixed((step, 2 * step))]
+        in_specs=[fixed((2 * step, step)), fixed((step, 2 * step)), fixed((2 * step, state_taps))]
         + [column(SLOT)] * 4
-        + [column(state_taps), column(1)],
+        + [column(2 * state_taps), column(1)],
         out_specs=[column(SLOT)] * 3 + [wide] * 3 + [column(2 * step)],
         out_shape=[shape((SLOT, channels), jnp.bfloat16)] * 3
         + [shape((2 * step, count * channels), jnp.bfloat16)] * 3
@@ -314,18 +320,17 @@
             pltpu.VMEM((step, count * width), jnp.bfloat16),
             pltpu.VMEM((2 * step, count * width), jnp.float32),
             pltpu.VMEM((2 * step, count * width), jnp.bfloat16),
+            pltpu.VMEM((SLOT, width), jnp.float32),
         ],
         compiler_params=pltpu.CompilerParams(vmem_limit_bytes=48 << 20),
         name="mix_forward",
-    )(forward_table, inverse_table, query, keys, values, kernel, taps, skip)
+    )(forward_table, inverse_table, low_table[:, :state_taps], query, keys, values, kernel, taps, skip)
 
 
 def run_backward(grad, query, values, saved, skip, state_taps):
     channels = query.shape[1]
     count, step, width = mixer_sizes(channels)
-    table = wave_table(step)
-    forward_table = jnp.asarray(table, jnp.bfloat16)
-    inverse_table = jnp.asarray(table.T / step, jnp.bfloat16)
+    forward_table, inverse_table, low_table = mixer_tables(step)
     fixed = lambda shape: pl.BlockSpec(shape, lambda j: (0, 0), pipeline_mode=pl.Buffered(1))
     column = lambda rows: pl.BlockSpec((rows, width), lambda j: (0, j))
     wide = pl.BlockSpec((2 * step, count * width), lambda j: (0, j))
@@ -358,6 +363,438 @@
         forward_table, inverse_table, grad, query, values, shifted, state,
         keys_hat, product_hat, kernel_hat, taps_hat, skip,
     )
+MESH = pl.DeviceIdType.MESH
+AXES = ("z", "y", "x")
+SIDES = ((0, 1), (1, -1))
+
+
+def chip_sizes(rows_axis, columns_axis):
+    across = columns_axis // 2
+    return {"z": rows_axis // across, "y": across, "x": across}
+
+
+def chip_place(sizes):
+    group, part = lax.axis_index("dp"), lax.axis_index("seq")
+    return {
+        "z": lax.div(group, sizes["y"]),
+        "y": lax.rem(group, sizes["y"]),
+        "x": lax.div(part, 2),
+        "core": lax.rem(part, 2),
+    }
+
+
+def device_at(sizes, place):
+    return {"dp": place["z"] * sizes["y"] + place["y"], "seq": place["x"] * 2 + place["core"]}
+
+
+def inside(value, size):
+    return jnp.logical_and(value >= 0, value < size)
+
+
+def meet(sizes, place):
+    barrier = pltpu.get_barrier_semaphore()
+    pl.semaphore_signal(
+        barrier,
+        inc=1,
+        device_id=device_at(sizes, {**place, "core": 1 - place["core"]}),
+        device_id_type=MESH,
+    )
+    count = jnp.int32(1)
+    for axis in AXES:
+        for step in (-1, 1):
+            other = place[axis] + step
+            there = inside(other, sizes[axis])
+            count = count + there.astype(jnp.int32)
+
+            @pl.when(there)
+            def _(axis=axis, other=other):
+                pl.semaphore_signal(
+                    barrier,
+                    inc=1,
+                    device_id=device_at(sizes, {**place, axis: other}),
+                    device_id_type=MESH,
+                )
+
+    pl.semaphore_wait(barrier, count)
+
+
+def plane_orders(sizes):
+    return (("x", "y"), ("y", "x"))
+
+
+def plane_hops(sizes):
+    return sizes["x"] + sizes["y"] - 2
+
+
+def plane_hop(sizes, order, number):
+    done = ()
+    for axis in order:
+        if number < sizes[axis] - 1:
+            return axis, done, number
+        number -= sizes[axis] - 1
+        done += (axis,)
+    return None
+
+
+def plane_index(place, wide, axis, value):
+    return tuple(
+        slice(None) if name in wide else (value if name == axis else place[name])
+        for name in ("y", "x")
+    )
+
+
+def gather_items(sizes, count):
+    return [
+        (k, step, side)
+        for k in range(count)
+        for step in range(sizes["z"])
+        for side in ((0,) if step == 0 else (0, 1))
+    ]
+
+
+def gather_kernel(sizes, count, *refs):
+    shards, fulls = refs[:count], refs[count : 2 * count]
+    send_sem, recv_sem, own_sem = refs[2 * count :]
+    place = chip_place(sizes)
+    core = place["core"]
+    meet(sizes, place)
+    items = gather_items(sizes, count)
+    last = plane_hops(sizes)
+
+    def own_copy(k):
+        target = fulls[k].at[place["z"], place["y"], place["x"], core]
+        return pltpu.make_async_copy(shards[k], target, own_sem.at[k])
+
+    def remote(block, item, number, side, target):
+        return pltpu.make_async_remote_copy(
+            src_ref=block,
+            dst_ref=block,
+            send_sem=send_sem.at[item, number, side],
+            recv_sem=recv_sem.at[item, number, side],
+            device_id=device_at(sizes, {**place, **target}),
+            device_id_type=MESH,
+        )
+
+    def layer(item):
+        k, step, side = items[item]
+        z = place["z"] - SIDES[side][1] * step
+        return k, z, inside(z, sizes["z"])
+
+    def along_z(item, act):
+        k, z, there = layer(item)
+        _, step, side = items[item]
+        block = fulls[k].at[z, place["y"], place["x"], core]
+        if act == "get" and step > 0:
+            direction = SIDES[side][1]
+
+            @pl.when(there)
+            def _():
+                remote(block, item, 0, side, {"z": place["z"] - direction}).wait_recv()
+
+        if act in ("send", "sent") and step < sizes["z"] - 1:
+            for out, direction in SIDES if step == 0 else (SIDES[side],):
+                target = place["z"] + direction
+                following = items.index((k, step + 1, out))
+
+                @pl.when(jnp.logical_and(there, inside(target, sizes["z"])))
+                def _():
+                    copy = remote(block, following, 0, out, {"z": target})
+                    copy.start() if act == "send" else copy.wait_send()
+
+    def in_plane(item, number, act):
+        k, z, there = layer(item)
+        for value, order in enumerate(plane_orders(sizes)):
+            axis, wide, before = plane_hop(sizes, order, number)
+            here, size = place[axis], sizes[axis]
+            for side, direction in SIDES:
+                if act == "get":
+                    held, other = here - direction * (before + 1), here - direction
+                    acts = inside(held, size)
+                else:
+                    held, other = here - direction * before, here + direction
+                    acts = jnp.logical_and(inside(held, size), inside(other, size))
+                acts = jnp.logical_and(jnp.logical_and(acts, there), core == value)
+
+                @pl.when(acts)
+                def _():
+                    block = fulls[k].at[(z,) + plane_index(place, wide, axis, held) + (core,)]
+                    copy = remote(block, item, 1 + number, side, {axis: other})
+                    if act == "send":
+                        copy.start()
+                    elif act == "sent":
+                        copy.wait_send()
+                    else:
+                        copy.wait_recv()
+
+    def across(item, act):
+        k, z, there = layer(item)
+
+        @pl.when(there)
+        def _():
+            owner = 1 - core if act == "get" else core
+            copy = remote(fulls[k].at[z, :, :, owner], item, 1 + last, 0, {"core": 1 - core})
+            if act == "send":
+                copy.start()
+            elif act == "sent":
+                copy.wait_send()
+            else:
+                copy.wait_recv()
+
+    for k in range(count):
+        own_copy(k).start()
+    for slot in range(len(items) + last):
+        for phase in range(last + 1):
+            item = slot - phase
+            if not 0 <= item < len(items):
+                continue
+            if phase == 0:
+                if items[item][1] == 0:
+                    own_copy(items[item][0]).wait()
+                along_z(item, "get")
+                along_z(item, "send")
+            else:
+                in_plane(item, phase - 1, "get")
+            if phase < last:
+                in_plane(item, phase, "send")
+            else:
+                across(item, "send")
+    for item in range(len(items)):
+        across(item, "get")
+        along_z(item, "sent")
+        for number in range(last):
+            in_plane(item, number, "sent")
+        across(item, "sent")
+
+
+def gather_all(arrays, sizes, collective_id):
+    lead = tuple(sizes[axis] for axis in AXES) + (2,)
+    count = len(arrays)
+    hbm = pl.BlockSpec(memory_space=pl.ANY)
+    semaphores = (len(gather_items(sizes, count)), plane_hops(sizes) + 2, 2)
+    fulls = pl.pallas_call(
+        functools.partial(gather_kernel, sizes, count),
+        out_shape=[jax.ShapeDtypeStruct(lead + a.shape, a.dtype) for a in arrays],
+        in_specs=[hbm] * count,
+        out_specs=[hbm] * count,
+        scratch_shapes=[
+            pltpu.SemaphoreType.DMA(semaphores),
+            pltpu.SemaphoreType.DMA(semaphores),
+            pltpu.SemaphoreType.DMA((count,)),
+        ],
+        compiler_params=pltpu.CompilerParams(
+            collective_id=collective_id, has_side_effects=True, vmem_limit_bytes=1 << 20
+        ),
+        name="gather_all",
+    )(*arrays)
+    return [f.reshape((-1,) + f.shape[5:]) for f in fulls]
+
+
+def reduce_items(sizes, count):
+    return [
+        (k, step, side)
+        for k in range(count)
+        for step in reversed(range(sizes["z"]))
+        for side in ((0,) if step == 0 else (0, 1))
+    ]
+
+
+def reduce_kernel(sizes, count, *refs):
+    grads, shares = refs[:count], refs[count : 2 * count]
+    rounded, sums, firsts = (refs[i * count : (i + 1) * count] for i in (2, 3, 4))
+    plane_in = refs[5 * count : 6 * count]
+    z_in = refs[6 * count : 7 * count]
+    send_sem, recv_sem, own_sem = refs[7 * count :]
+    place = chip_place(sizes)
+    core = place["core"]
+    meet(sizes, place)
+    items = reduce_items(sizes, count)
+    last = plane_hops(sizes)
+
+    def layer(item):
+        k, step, side = items[item]
+        z = place["z"] + SIDES[side][1] * step
+        return k, z, inside(z, sizes["z"])
+
+    def remote(source, landing, item, number, side, target):
+        return pltpu.make_async_remote_copy(
+            src_ref=source,
+            dst_ref=landing,
+            send_sem=send_sem.at[item, number, side],
+            recv_sem=recv_sem.at[item, number, side],
+            device_id=device_at(sizes, {**place, **target}),
+            device_id_type=MESH,
+        )
+
+    def own_copy(item):
+        k, z, _ = layer(item)
+        return pltpu.make_async_copy(
+            grads[k].at[z, :, :, core], rounded[k].at[z], own_sem.at[item]
+        )
+
+    def across(item):
+        k, z, _ = layer(item)
+        return remote(
+            grads[k].at[z, :, :, 1 - core], firsts[k].at[z], item, 0, 0, {"core": 1 - core}
+        )
+
+    def begin(item):
+        @pl.when(layer(item)[2])
+        def _():
+            own_copy(item).start()
+            across(item).start()
+
+    def put(k, index, total):
+        sums[k][index] = total
+        rounded[k][index] = total.astype(jnp.bfloat16)
+
+    def join_cores(item):
+        k, z, there = layer(item)
+
+        @pl.when(there)
+        def _():
+            own_copy(item).wait()
+            across(item).wait_recv()
+
+            @pl.loop(0, sizes["y"] * sizes["x"])
+            def _(flat):
+                index = (z, lax.div(flat, sizes["x"]), lax.rem(flat, sizes["x"]))
+                put(
+                    k,
+                    index,
+                    rounded[k][index].astype(jnp.float32) + firsts[k][index].astype(jnp.float32),
+                )
+
+    def in_plane(item, number, act):
+        k, z, there = layer(item)
+        for value, order in enumerate(plane_orders(sizes)):
+            axis, wide, step = plane_hop(sizes, order, number)
+            wide = tuple(name for name in order[order.index(axis) + 1 :])
+            here, size = place[axis], sizes[axis]
+            far = size - 1 - step
+            spans = int(np.prod([sizes[name] for name in wide], dtype=np.int64))
+            for side, direction in SIDES:
+                if act == "get":
+                    other = here - direction
+                    goal = other + direction * far
+                    acts = jnp.logical_and(inside(other, size), inside(goal, size))
+                else:
+                    other = here + direction
+                    goal = here + direction * far
+                    acts = inside(goal, size)
+                acts = jnp.logical_and(jnp.logical_and(acts, there), core == value)
+
+                @pl.when(acts)
+                def _():
+                    source = rounded[k].at[(z,) + plane_index(place, wide, axis, goal)]
+                    landing = plane_in[k].at[z, number, side]
+                    landing = landing.at[pl.ds(0, spans)] if wide else landing.at[0]
+                    copy = remote(source, landing, item, 1 + number, side, {axis: other})
+                    if act == "send":
+                        copy.start()
+                    elif act == "sent":
+                        copy.wait_send()
+                    else:
+                        copy.wait_recv()
+
+                        @pl.loop(0, spans)
+                        def _(flat):
+                            at = {name: flat for name in wide}
+                            at[axis] = goal
+                            index = (z,) + tuple(at.get(name, place[name]) for name in ("y", "x"))
+                            came = plane_in[k][z, number, side, flat].astype(jnp.float32)
+                            put(k, index, sums[k][index] + came)
+
+    def along_z(item, act):
+        k, z, there = layer(item)
+        _, step, side = items[item]
+        index = (z, place["y"], place["x"])
+        if act == "get":
+            for out, direction in SIDES if step == 0 else (SIDES[side],):
+                other = place["z"] - direction
+
+                @pl.when(jnp.logical_and(there, inside(other, sizes["z"])))
+                def _():
+                    if step + 1 < sizes["z"]:
+                        leaving = items.index((k, step + 1, out))
+                        remote(
+                            rounded[k].at[index], z_in[k].at[out, step], leaving, 1 + last, 0,
+                            {"z": other},
+                        ).wait_recv()
+                        put(
+                            k, index, sums[k][index] + z_in[k][out, step].astype(jnp.float32)
+                        )
+
+            if step == 0:
+                shares[k][...] = sums[k][index]
+        elif step > 0:
+            direction = SIDES[side][1]
+
+            @pl.when(there)
+            def _():
+                copy = remote(
+                    rounded[k].at[index], z_in[k].at[side, step - 1], item, 1 + last, 0,
+                    {"z": place["z"] + direction},
+                )
+                copy.start() if act == "send" else copy.wait_send()
+
+    for item in range(len(items)):
+        begin(item)
+    for slot in range(len(items) + last + 1):
+        for phase in range(last + 2):
+            item = slot - phase
+            if not 0 <= item < len(items):
+                continue
+            if phase == 0:
+                join_cores(item)
+            elif phase <= last:
+                in_plane(item, phase - 1, "get")
+            if phase < last:
+                in_plane(item, phase, "send")
+            if phase == last + 1:
+                along_z(item, "get")
+                along_z(item, "send")
+    for item in range(len(items)):
+
+        @pl.when(layer(item)[2])
+        def _():
+            across(item).wait_send()
+
+        for number in range(last):
+            in_plane(item, number, "sent")
+        along_z(item, "sent")
+
+
+def reduce_all(arrays, sizes, collective_id):
+    lead = tuple(sizes[axis] for axis in AXES)
+    devices = 2 * int(np.prod(lead))
+    count = len(arrays)
+    blocks = [(a.shape[0] // devices, a.shape[1]) for a in arrays]
+    views = [
+        a.astype(jnp.bfloat16).reshape(lead + (2,) + block) for a, block in zip(arrays, blocks)
+    ]
+    last = plane_hops(sizes)
+    widest = max(sizes["x"], sizes["y"])
+    semaphores = (len(reduce_items(sizes, count)), last + 2, 2)
+    return pl.pallas_call(
+        functools.partial(reduce_kernel, sizes, count),
+        out_shape=[jax.ShapeDtypeStruct(block, jnp.float32) for block in blocks],
+        in_specs=[pl.BlockSpec(memory_space=pl.ANY)] * count,
+        out_specs=[pl.BlockSpec(memory_space=pltpu.VMEM)] * count,
+        scratch_shapes=[pltpu.VMEM(lead + block, jnp.bfloat16) for block in blocks]
+        + [pltpu.VMEM(lead + block, jnp.float32) for block in blocks]
+        + [pltpu.VMEM(lead + block, jnp.bfloat16) for block in blocks]
+        + [pltpu.VMEM((sizes["z"], last, 2, widest) + block, jnp.bfloat16) for block in blocks]
+        + [pltpu.VMEM((2, sizes["z"]) + block, jnp.bfloat16) for block in blocks]
+        + [
+            pltpu.SemaphoreType.DMA(semaphores),
+            pltpu.SemaphoreType.DMA(semaphores),
+            pltpu.SemaphoreType.DMA((semaphores[0],)),
+        ],
+        compiler_params=pltpu.CompilerParams(
+            collective_id=collective_id, has_side_effects=True, vmem_limit_bytes=60 << 20
+        ),
+        name="reduce_all",
+    )(*views)
 
 
 def powers(rate, turn, count, stride):
@@ -430,10 +867,7 @@
     slot, rank = place // half, place % half
     channels = width // half
     state_taps = shift_taps.shape[1]
-    gather = functools.partial(lax.all_gather, axis_name=both, axis=0, tiled=True)
-    scatter = functools.partial(
-        lax.psum_scatter, axis_name=both, scatter_dimension=0, tiled=True
-    )
+    sizes = chip_sizes(lax.axis_size("dp"), parts)
 
     def swap(values):
         return lax.ppermute(values, "seq", [(i, (i + half) % parts) for i in range(parts)])
@@ -456,34 +890,37 @@
         )
 
     token_rows = rows_of(tokens)
-    cot_rows = rows_of(cotangent)
-    qkv_full = gather(qkv_weight)
     gain_high, gain_low = two_parts(norm_gains)
     skip_high, skip_low = two_parts(skip_gain[:, None])
+    taps_high, taps_low = two_parts(shift_taps)
     kernel_own = mode_kernel(decay_rate, frequency, mode_coef)
     small = jnp.concatenate(
         [
             kernel_own.astype(jnp.bfloat16),
-            shift_taps.astype(jnp.bfloat16),
+            taps_high,
+            taps_low,
             gain_high,
             gain_low,
             skip_high,
             skip_low,
-            jnp.zeros((kernel_own.shape[0], 58), jnp.bfloat16),
+            jnp.zeros((kernel_own.shape[0], 128 - 6), jnp.bfloat16),
         ],
         axis=1,
     )
-    small_full = gather(small)
-    out_full = gather(out_weight)
-    up_full = gather(up_weight)
-    down_full = gather(down_weight)
+    qkv_full, small_full, out_full, up_full, down_full = gather_all(
+        [qkv_weight, small, out_weight, up_weight, down_weight],
+        sizes,
+        0,
+    )
+    cotangent, down_full = lax.optimization_barrier((cotangent, down_full))
+    cot_rows = rows_of(cotangent)
     base = SLOT + state_taps
-    extra = small_full[:, base : base + 6].astype(jnp.float32)
+    extra = small_full[:, base + state_taps : base + state_taps + 6].astype(jnp.float32)
     gain_one, gain_two = extra[:, 0] + extra[:, 2], extra[:, 1] + extra[:, 3]
     start = rank * channels
     mine = lax.dynamic_slice_in_dim(small_full, start, channels, 0)
     kernel_mine = mine[:, :SLOT].T
-    taps_mine = mine[:, SLOT:base].T
+    taps_mine = mine[:, SLOT : base + state_taps].T
     skip_mine = lax.dynamic_slice_in_dim(extra[:, 4] + extra[:, 5], start, channels, 0)[None, :]
 
     input_rows = token_rows.astype(jnp.float32)
@@ -553,8 +990,7 @@
     grad_normed = mat_dot(grad_pre, up_full, ((1,), (1,)))
     grad_hidden_norm, grad_gain_two = norm_two_back(grad_normed)
     grad_hidden = grad_sum + grad_hidden_norm
-    up_share = scatter(up_grad)
-    down_share = scatter(down_grad)
+    up_share, down_share = reduce_all([up_grad, down_grad], sizes, 1)
     grad_mix = grad_hidden.astype(jnp.bfloat16)
     out_grad = mat_dot(mixed_rows, grad_mix, ((0,), (0,)))
     grad_mixed = mat_dot(grad_mix, out_full, ((1,), (1,))).astype(jnp.bfloat16)
@@ -574,7 +1010,9 @@
     )
     wide = jnp.concatenate([wide, grad_gain_one[:, None], grad_gain_two[:, None]], axis=1)
     wide = jnp.pad(wide, ((0, 0), (0, -wide.shape[1] % 128)))
-    qkv_share, out_share, small_share = scatter(qkv_grad), scatter(out_grad), scatter(wide)
+    out_share, small_share, qkv_share = reduce_all(
+        [out_grad, wide, qkv_grad], sizes, 2
+    )
     grad_rate, grad_turn, grad_coef = mode_grads(
         decay_rate, frequency, mode_coef, small_share[:, :SLOT]
     )

time: 1140 us -> 616 us (0.54)
  waiting for transfers between devices: 782 us -> 3.24 us
  Pallas kernels: 63.4 us -> 331 us
  matrix products: 134 us -> 117 us
  between operations: 15.5 us -> 1.85 us
  local copies, waits for them, and re-layouts: 86.4 us -> 98 us
    reduce_scatter x4 -> x0, waiting for transfers between devices: 502 us -> none  [the longest x1 142 us: local(): down_share = scatter(down_grad)]
    pallas_call x0 -> x3, Pallas kernels: none -> 268 us  [the longest x2 142 us: reduce_all(): pl.pallas_call(functools.partial(reduce_kernel, sizes, count), out_shape=...]
    all_gather x5 -> x0, waiting for transfers between devices: 156 us -> none  [the longest x1 60 us: local(): qkv_full = gather(qkv_weight)]
    unnamed x11 -> x0, waiting for transfers between devices: 73.3 us -> none
    ppermute x4, waiting for transfers between devices: 49.6 us -> 3.23 us  [swap(): lax.ppermute(values, 'seq', [(i, (i + half) % parts) for i in range(parts)])]
    unnamed x118 -> x176, local copies, waits for them, and re-layouts: 13.4 us -> 31.7 us
    dot_general x12, matrix products: 131 us -> 114 us  [mat_dot(): lax.dot_general(left, right, (contract, ((), ())), preferred_element_type...]
  transfers between devices with their start and end apart: 18 -> 8, of which waited for: 13 -> 1; matrix products, arithmetic and copies ran while one was open for 16% -> 13% of each run, Pallas kernels for 3% -> 42%
where the time goes in v2:
time: 616 us; the launch traced here: 611 us
  Pallas kernels  331 us (54%)
  matrix products  117 us (19%)
  local copies, waits for them, and re-layouts  98 us (16%)
  other arithmetic  51.8 us (8%)
  starting transfers between devices  6.92 us (1%)
    pallas_call x2, Pallas kernels, reduce_all(): pl.pallas_call(functools.partial(reduce_kernel, sizes, count), out_shape=...  142 us
    pallas_call x1, Pallas kernels, gather_all(): pl.pallas_call(functools.partial(gather_kernel, sizes, count), out_shape=...  126 us
    dot_general x12, matrix products, mat_dot(): lax.dot_general(left, right, (contract, ((), ())), preferred_element_type...  114 us
    pallas_call x1, Pallas kernels, run_backward(): pl.pallas_call(functools.partial(mix_backward, count, step, width), grid=...  33.8 us
    unnamed x176, local copies, waits for them, and re-layouts  31.7 us
    pallas_call x1, Pallas kernels, run_forward(): pl.pallas_call(functools.partial(mix_forward, count, step, width), grid=(...  29.7 us
    dynamic_slice x2, local copies, waits for them, and re-layouts, to_channels(): lax.dynamic_index_in_dim(by_rank, (rank + k) % half, 2, keepdims=False)  13.5 us
  transfers between devices with their start and end apart: 8, of which 1 were waited for; matrix products, arithmetic and copies ran while one was open for 13% of the time, Pallas kernels for 42%

profile of v2, /device:TPU:0, one launch (start us, length us, event | category | flops | bytes accessed | tf_op | source)
XLA Modules:
  0.0 610.6 jit_solution(9738316375973996430)
XLA Ops:
  2.8 2.9 collective-permute-start
  8.8 3.2 broadcast_multiply_fusion.1
  20.3 125.8 %gather_all.1 = (bf16[4,2,2,2,24,2304]{5,4,3,2,1,0:T(8,128)(2,1)S(1)}, bf16[4,2,2,2,24,2304]{5,4,3,2,1,0:T(8,128)(2,1)S(1)}, bf16[4,2,2,2,24,768]{5,4,3,2,1,0:T(...) custom-call(bf16[24,2304]{1,0:T(8,128)(2,1)S(1)} %copy-done.9, ...), custom_call_target="tpu_custom_call" | custom-call | tf_op jit(solution)/shard_map/gather_all/pallas_call | solution.py:574
  148.2 2.2 copy-done.12
  157.0 6.6 %convolution_convert_fusion = bf16[1024,2304]{1,0:T(8,128)(2,1)} fusion(bf16[768,2304]{1,0:T(8,128)(2,1)S(1)} %bitcast.147, f32[768]{0:T(1024)S(1)} %get-tuple-element.145, f32[1024]{0:T(1024)S(1)} %fusion.47, f32[1024]{0:T(1024)S(1)} %broadcast_multiply_fusion.3, bf16[512,768]{1,0:T(8,128)(2,1)S(1)} %get-tuple-element.134, ...), kind=kOutput, calls=%fused_computation.17 | convolution fusion | flops 3632529408 | bytes 9841664 | tf_op jit(solution)/shard_map/dot_general | solution.py:28
  163.6 9.9 %reshape.247 = bf16[1024,3,2,384]{3,2,1,0:T(2,128)(2,1)} reshape(bf16[1024,2304]{1,0:T(8,128)(2,1)} %convolution_convert_fusion) | data formatting | bytes 9437184 | tf_op jit(solution)/shard_map/reshape | solution.py:937
  173.5 12.2 %constant_dynamic-slice_fusion.8 = (bf16[1024,3,1,384]{3,2,1,0:T(2,128)(2,1)}, bf16[1024,3,1,384]{3,2,1,0:T(2,128)(2,1)S(1)}) fusion(bf16[1024,3,2,384]{3,2,1,0:T(2,128)(2,1)} %reshape.247, s32[]{:T(128)S(6)} %select_n.190, s32[]{:T(128)S(6)} %select_n.192), kind=kLoop, calls=%fused_computation.145 | loop fusion | bytes 9437192 | tf_op jit(solution)/shard_map/jit(dynamic_index_in_dim)/dynamic_slice | solution.py:940
  193.0 2.8 copy.88
  197.5 3.7 broadcast_select_fusion.1
  201.8 2.3 slice_bitcast_fusion
  204.6 29.7 %mix_forward.1 = (bf16[2048,384]{1,0:T(8,128)(2,1)S(1)}, bf16[2048,384]{1,0:T(8,128)(2,1)S(1)}, bf16[2048,384]{1,0:T(8,128)(2,1)}, bf16[1024,1536]{1,0:T(8,128)(...) custom-call(bf16[1024,512]{1,0:T(8,128)(2,1)S(1)} %copy-done, ...), custom_call_target="tpu_custom_call" | custom-call | tf_op jit(solution)/shard_map/mix_forward/pallas_call | solution.py:309
  245.1 34.8 %multiply_convert_fusion = (bf16[1024,3072]{1,0:T(8,128)(2,1)}, f32[1024,3072]{1,0:T(8,128)}, f32[1024,3072]{1,0:T(8,128)}) fusion(bf16[768,3072]{1,0:T(8,128)(2,1)S(1)} %bitcast.146, f32[1024,768]{1,0:T(8,128)S(1)} %get-tuple-element.160, f32[768]{0:T(1024)S(1)} %get-tuple-element.146, f32[1024]{0:T(1024)S(1)} %fusion.48, f32[1024]{0:T(1024)S(1)} %broadcast_multiply_fusion.2), kind=kOutput, calls=%fused_computation.3 | convolution fusion | flops 5039456256 | bytes 39332864 | tf_op jit(solution)/shard_map/dot_general | solution.py:28
  279.9 17.2 %add_convert_fusion = bf16[1024,3072]{1,0:T(8,128)(2,1)} fusion(f32[1024,3072]{1,0:T(8,128)} %get-tuple-element.111, f32[1024,3072]{1,0:T(8,128)} %get-tuple-element.161, bf16[3072,768]{1,0:T(8,128)(2,1)} %bitcast.141, f32[1024]{0:T(1024)S(1)} %fusion.46, bf16[512,768]{1,0:T(8,128)(2,1)S(1)} %get-tuple-element.130, bf16[512,768]{1,0:T(8,128)(2,1)S(1)} %get-tuple-element.129), kind=kOutput, calls=%fused_computation.2 | convolution fusion | flops 4880596992 | bytes 37752832 | tf_op jit(solution)/shard_map/dot_general | solution.py:28
  297.1 10.3 %convolution_convert_fusion.2 = bf16[768,3072]{1,0:T(8,128)(2,1)} fusion(bf16[1024,3072]{1,0:T(8,128)(2,1)} %add_convert_fusion, f32[1024,768]{1,0:T(8,128)} %copy-done.25, f32[768]{0:T(1024)S(1)} %get-tuple-element.146, f32[1024]{0:T(1024)S(1)} %fusion.48, f32[1024]{0:T(1024)S(1)} %broadcast_multiply_fusion.2), kind=kOutput, calls=%fused_computation.19 | convolution fusion | flops 4837343232 | bytes 14167040 | tf_op jit(solution)/shard_map/dot_general | solution.py:28
  307.4 7.9 %multiply_reduce_fusion = (bf16[768]{0:T(1024)(128)(2,1)S(1)}, f32[1024]{0:T(1024)S(1)}, f32[1024,768]{1,0:T(8,128)S(1)}) fusion(f32[1024,768]{1,0:T(8,128)S(1)} %copy-done.26, f32[1024]{0:T(1024)S(1)} %fusion.48, f32[1024]{0:T(1024)S(1)} %broadcast_multiply_fusion.2, f32[768]{0:T(1024)S(1)} %get-tuple-element.146, bf16[1024,3072]{1,0:T(8,128)(2,1)S(1)} %copy-done.78, ...), kind=kOutput, calls=%fused_computation.41 | convolution fusion | flops 4837341184 | bytes 17318400 | tf_op jit(solution)/shard_map/dot_general | solution.py:28
  321.3 2.5 copy.91
  324.4 9.4 %add_multiply_fusion = bf16[1024,768]{1,0:T(8,128)(2,1)} fusion(f32[1024,768]{1,0:T(8,128)S(1)} %copy-done.27, bf16[1024,3072]{1,0:T(8,128)(2,1)} %get-tuple-element.110, bf16[3072,768]{1,0:T(8,128)(2,1)} %bitcast.142, f32[1024]{0:T(1024)S(1)} %fusion.46), kind=kOutput, calls=%fused_computation.47 | convolution fusion | flops 4834197504 | bytes 15732736 | tf_op jit(solution)/shard_map/dot_general | solution.py:28
  339.8 33.8 %mix_backward.1 = (bf16[2048,384]{1,0:T(8,128)(2,1)S(1)}, bf16[2048,384]{1,0:T(8,128)(2,1)S(1)}, bf16[2048,384]{1,0:T(8,128)(2,1)}, f32[2048,384]{1,0:T(8,128)},...) custom-call(bf16[1024,512]{1,0:T(8,128)(2,1)S(1)} %copy-done.1, bf16[512,1024]{1,0:T(8,128)(2,1)S(1)} %copy-done.3, ...), custom_call_target="tpu_custom_call" | custom-call | tf_op jit(solution)/shard_map/mix_backward/pallas_call | solution.py:339
  379.2 7.3 %convolution_convert_fusion.1 = bf16[3072,768]{1,0:T(8,128)(2,1)} fusion(bf16[1024,3072]{1,0:T(8,128)(2,1)S(1)} %bitcast.180, f32[1024]{0:T(1024)S(1)} %fusion.46, bf16[512,768]{1,0:T(8,128)(2,1)S(1)} %copy-done.34, bf16[512,768]{1,0:T(8,128)(2,1)S(1)} %copy-done.32), kind=kOutput, calls=%fused_computation.18 | convolution fusion | flops 4838916096 | bytes 12587008 | tf_op jit(solution)/shard_map/dot_general | solution.py:28
  386.4 67.2 %reduce_all.3 = (f32[24,3072]{1,0:T(8,128)}, f32[96,768]{1,0:T(8,128)}) custom-call(bf16[4,2,2,2,24,3072]{5,4,3,2,1,0:T(8,128)(2,1)} %bitcast.159, bf16[4,2,2,2,96,768]{5,4,3,2,1,0:T(8,128)(2,1)} %bitcast.162), custom_call_target="tpu_custom_call" | custom-call | tf_op jit(solution)/shard_map/reduce_all/pallas_call | solution.py:778
  453.8 4.5 convolution_convert_fusion.5
  459.7 4.1 copy.77
  472.1 2.6 pad_maximum_fusion.2
  474.6 6.8 %copy.76 = bf16[1024,3,768]{0,2,1:T(8,128)(2,1)} copy(bf16[1024,3,768]{2,0,1:T(8,128)(2,1)} %pad_maximum_fusion.2) | data formatting | bytes 9437184 | tf_op jit(solution)/shard_map/concatenate | solution.py:963
  481.5 8.5 %convolution_convert_fusion.3 = bf16[768,2304]{1,0:T(8,128)(2,1)} fusion(bf16[1024,2304]{0,1:T(8,128)(2,1)} %bitcast.160, f32[768]{0:T(1024)S(1)} %copy-done.64, f32[1024]{0:T(1024)S(1)} %copy-done.66, f32[1024]{0:T(1024)S(1)} %copy-done.62, bf16[512,768]{1,0:T(8,128)(2,1)S(1)} %copy-done.24, bf16[512,768]{1,0:T(8,128)(2,1)S(1)} %copy-done.21), kind=kOutput, calls=%fused_computation.20 | convolution fusion | flops 3631939584 | bytes 9841664 | tf_op jit(solution)/shard_map/dot_general | solution.py:28
  490.0 4.5 fusion.15
  494.6 3.2 fusion.13
  498.6 4.9 concatenate.50
  505.5 74.9 %reduce_all.2 = (f32[24,768]{1,0:T(8,128)}, f32[24,2176]{1,0:T(8,128)}, f32[24,2304]{1,0:T(8,128)}) custom-call(bf16[4,2,2,2,24,768]{5,4,3,2,1,0:T(8,128)(2,1)} %bitcast.170, bf16[4,2,2,2,24,2176]{5,4,3,2,1,0:T(8,128)(2,1)} %bitcast.152, bf16[4,2,2,2,24,2304]{5,4,3,2,1,0:T(8,128)(2,1)} %bitcast.163), custom_call_target="tpu_custom_call" | custom-call | tf_op jit(solution)/shard_map/reduce_all/pallas_call | solution.py:778
  584.5 4.9 add_add_fusion.2
  593.0 2.6 fusion.20
  601.1 3.2 collective-permute-done.7
  (264 shorter events, 92.2 us)
Async XLA Ops:
  0.6 11.4 %copy-start.56 = (f32[24,32]{1,0:T(8,128)S(1)}, f32[24,32]{1,0:T(8,128)}, u32[]{:S(2)}) copy-start(f32[24,32]{1,0:T(8,128)} %param.24) | copy-start | bytes 9220
  0.7 14.5 %copy-start.74 = (f32[24,64]{1,0:T(8,128)S(1)}, f32[24,64]{1,0:T(8,128)}, u32[]{:S(2)}) copy-start(f32[24,64]{1,0:T(8,128)} %param.22) | copy-start | bytes 18436
  2.8 150.6 %collective-permute-start = (bf16[512,768]{1,0:T(8,128)(2,1)}, bf16[512,768]{1,0:T(8,128)(2,1)}, u32[]{:S(2)}, u32[]{:S(2)}) collective-permute-start(bf16[512,768]{1,0:T(8,128)(2,1)} %dynamic-slice_bitcast_fusion.1), channel_id=1, source_target_pairs={{0,2},{1,3},{2,0},{3,1},{4,6},{5,7},{6,4},{7,5},{8,10},{9,11},{10,... | collective-permute-start | bytes 2359304 | tf_op jit(solution)/shard_map/ppermute | solution.py:873
  5.7 7.9 %copy-start.75 = (f32[32]{0:T(128)}, f32[32]{0:T(128)S(1)}, u32[]{:S(2)}) copy-start(f32[32]{0:T(128)S(1)} %multiply_convert_fusion.2) | copy-start | bytes 388
  6.5 7.1 %copy-start.54 = (f32[24,1,32]{2,1,0:T(1,128)}, f32[24,1,32]{2,1,0:T(1,128)S(1)}, u32[]{:S(2)}) copy-start(f32[24,1,32]{2,1,0:T(1,128)S(1)} %get-tuple-element.156) | copy-start | bytes 9220
  187.5 10.0 %collective-permute-start.1 = (bf16[1024,3,384]{2,0,1:T(8,128)(2,1)}, bf16[1024,3,384]{2,0,1:T(8,128)(2,1)}, u32[]{:S(2)}, u32[]{:S(2)}) collective-permute-start(bf16[1024,3,384]{2,0,1:T(8,128)(2,1)} %bitcast.133), channel_id=1, source_target_pairs={{0,1},{1,0},{2,3},{3,2},{4,5},{5,4},{6,7},{7,6},{8,9},{9,8},{10,11... | collective-permute-start | bytes 7077896 | tf_op jit(solution)/shard_map/ppermute | solution.py:933
  188.9 48.9 %collective-permute-start.4 = (bf16[512,768]{1,0:T(8,128)(2,1)}, bf16[512,768]{1,0:T(8,128)(2,1)}, u32[]{:S(2)}, u32[]{:S(2)}) collective-permute-start(bf16[512,768]{1,0:T(8,128)(2,1)} %dynamic-slice_bitcast_fusion), channel_id=1, source_target_pairs={{0,2},{1,3},{2,0},{3,1},{4,6},{5,7},{6,4},{7,5},{8,10},{9,11},{10,... | collective-permute-start | bytes 2359304 | tf_op jit(solution)/shard_map/ppermute | solution.py:873
  236.5 3.0 collective-permute-start.2
  237.7 139.9 %copy-start.67 = (f32[1024]{0:T(1024)}, f32[1024]{0:T(1024)S(1)}, u32[]{:S(2)}) copy-start(f32[1024]{0:T(1024)S(1)} %fusion.46) | copy-start | bytes 12292
  239.4 77.6 %copy-start.31 = (bf16[512,768]{1,0:T(8,128)(2,1)}, bf16[512,768]{1,0:T(8,128)(2,1)S(1)}, u32[]{:S(2)}) copy-start(bf16[512,768]{1,0:T(8,128)(2,1)S(1)} %get-tuple-element.129) | copy-start | bytes 2359300
  239.4 77.6 %copy-start.33 = (bf16[512,768]{1,0:T(8,128)(2,1)}, bf16[512,768]{1,0:T(8,128)(2,1)S(1)}, u32[]{:S(2)}) copy-start(bf16[512,768]{1,0:T(8,128)(2,1)S(1)} %get-tuple-element.130) | copy-start | bytes 2359300
  242.9 37.0 %copy-start.25 = (f32[1024,768]{1,0:T(8,128)}, f32[1024,768]{1,0:T(8,128)S(1)}, u32[]{:S(2)}) copy-start(f32[1024,768]{1,0:T(8,128)S(1)} %get-tuple-element.160) | copy-start | bytes 9437188
  297.1 10.3 %copy-start.26 = (f32[1024,768]{1,0:T(8,128)S(1)}, f32[1024,768]{1,0:T(8,128)}, u32[]{:S(2)}) copy-start(f32[1024,768]{1,0:T(8,128)} %copy-done.25) | copy-start | bytes 9437188
  297.1 10.3 %copy-start.78 = (bf16[1024,3072]{1,0:T(8,128)(2,1)S(1)}, bf16[1024,3072]{1,0:T(8,128)(2,1)}, u32[]{:S(2)}) copy-start(bf16[1024,3072]{1,0:T(8,128)(2,1)} %add_convert_fusion) | copy-start | bytes 18874372
  323.9 13.1 %collective-permute-start.5 = (bf16[1024,1,384]{2,0,1:T(8,128)(2,1)}, bf16[1024,1,384]{2,0,1:T(8,128)(2,1)}, u32[]{:S(2)}, u32[]{:S(2)}) collective-permute-start(bf16[1024,1,384]{2,0,1:T(8,128)(2,1)} %bitcast.171), channel_id=1, source_target_pairs={{0,1},{1,0},{2,3},{3,2},{4,5},{5,4},{6,7},{7,6},{8,9},{9,8},{10,11... | collective-permute-start | bytes 2359304 | tf_op jit(solution)/shard_map/ppermute | solution.py:933
  336.5 127.3 %collective-permute-start.3 = (bf16[512,768]{1,0:T(8,128)(2,1)S(1)}, bf16[512,768]{1,0:T(8,128)(2,1)}, u32[]{:S(2)}, u32[]{:S(2)}) collective-permute-start(bf16[512,768]{1,0:T(8,128)(2,1)S(1)} %fusion.29), channel_id=1, source_target_pairs={{0,2},{1,3},{2,0},{3,1},{4,6},{5,7},{6,4},{7,5},{8,10},{9,11},{10,... | collective-permute-start | bytes 2359304 | tf_op jit(solution)/shard_map/ppermute | solution.py:873
  377.6 92.4 %collective-permute-start.6 = (bf16[1024,3,384]{2,0,1:T(8,128)(2,1)}, bf16[1024,3,384]{2,0,1:T(8,128)(2,1)}, u32[]{:S(2)}, u32[]{:S(2)}) collective-permute-start(bf16[1024,3,384]{2,0,1:T(8,128)(2,1)} %bitcast.50), channel_id=1, source_target_pairs={{0,1},{1,0},{2,3},{3,2},{4,5},{5,4},{6,7},{7,6},{8,9},{9,8},{10,11... | collective-permute-start | bytes 7077896 | tf_op jit(solution)/shard_map/ppermute | solution.py:933
  481.5 8.6 %copy-start.14 = (bf16[4,2,2,2,24,2304]{5,4,3,2,1,0:T(8,128)(2,1)S(1)}, bf16[4,2,2,2,24,2304]{5,4,3,2,1,0:T(8,128)(2,1)}, u32[]{:S(2)}) copy-start(bf16[4,2,2,2,24,2304]{5,4,3,2,1,0:T(8,128)(2,1)} %copy-done.13) | copy-start | bytes 10616836
  481.5 8.6 %copy-start.36 = (bf16[1024,3,768]{0,2,1:T(8,128)(2,1)S(1)}, bf16[1024,3,768]{0,2,1:T(8,128)(2,1)}, u32[]{:S(2)}) copy-start(bf16[1024,3,768]{0,2,1:T(8,128)(2,1)} %copy.76) | copy-start | bytes 14155780
  505.5 78.9 %copy-start.73 = (f32[1024]{0:T(1024)S(1)}, f32[1024]{0:T(1024)}, u32[]{:S(2)}) copy-start(f32[1024]{0:T(1024)} %get-tuple-element.101) | copy-start | bytes 12292
  505.5 78.9 %copy-start.18 = (f32[1024,768]{1,0:T(8,128)S(1)}, f32[1024,768]{1,0:T(8,128)}, u32[]{:S(2)}) copy-start(f32[1024,768]{1,0:T(8,128)} %copy-done.17) | copy-start | bytes 9437188
  505.5 78.9 %copy-start.68 = (f32[1024]{0:T(1024)S(1)}, f32[1024]{0:T(1024)}, u32[]{:S(2)}) copy-start(f32[1024]{0:T(1024)} %copy-done.67) | copy-start | bytes 12292
  505.5 78.9 %copy-start.70 = (f32[1024]{0:T(1024)S(1)}, f32[1024]{0:T(1024)}, u32[]{:S(2)}) copy-start(f32[1024]{0:T(1024)} %copy-done.69) | copy-start | bytes 12292
  584.4 8.6 %copy-start.39 = (f32[24,32,64]{2,1,0:T(8,128)S(1)}, f32[24,32,64]{2,1,0:T(8,128)}, u32[]{:S(2)}) copy-start(f32[24,32,64]{2,1,0:T(8,128)} %copy-done.38) | copy-start | bytes 589828
  584.4 8.6 %copy-start.41 = (f32[24,32,64]{2,1,0:T(8,128)S(1)}, f32[24,32,64]{2,1,0:T(8,128)}, u32[]{:S(2)}) copy-start(f32[24,32,64]{2,1,0:T(8,128)} %copy-done.40) | copy-start | bytes 589828
  584.4 8.6 %copy-start.46 = (f32[24,32,64]{2,1,0:T(8,128)S(1)}, f32[24,32,64]{2,1,0:T(8,128)}, u32[]{:S(2)}) copy-start(f32[24,32,64]{2,1,0:T(8,128)} %reshape.265) | copy-start | bytes 589828
  584.4 8.6 %copy-start.47 = (f32[24,32,64]{2,1,0:T(8,128)S(1)}, f32[24,32,64]{2,1,0:T(8,128)}, u32[]{:S(2)}) copy-start(f32[24,32,64]{2,1,0:T(8,128)} %get-tuple-element.151) | copy-start | bytes 589828
  584.5 8.6 %copy-start.48 = (f32[24,32,64]{2,1,0:T(8,128)S(1)}, f32[24,32,64]{2,1,0:T(8,128)}, u32[]{:S(2)}) copy-start(f32[24,32,64]{2,1,0:T(8,128)} %get-tuple-element.153) | copy-start | bytes 589828
  591.0 9.5 %copy-start.55 = (f32[24,1,32]{2,1,0:T(1,128)S(1)}, f32[24,1,32]{2,1,0:T(1,128)}, u32[]{:S(2)}) copy-start(f32[24,1,32]{2,1,0:T(1,128)} %copy-done.54) | copy-start | bytes 9220
  591.0 9.5 %copy-start.59 = (f32[24,1,32]{2,1,0:T(1,128)S(1)}, f32[24,1,32]{2,1,0:T(1,128)}, u32[]{:S(2)}) copy-start(f32[24,1,32]{2,1,0:T(1,128)} %copy-done.58) | copy-start | bytes 9220
  592.0 12.3 %copy-start.30 = (f32[1024,768]{1,0:T(8,128)S(1)}, f32[1024,768]{1,0:T(8,128)}, u32[]{:S(2)}) copy-start(f32[1024,768]{1,0:T(8,128)} %copy-done.29) | copy-start | bytes 9437188
  592.0 12.3 %collective-permute-start.7 = (bf16[512,768]{1,0:T(8,128)(2,1)}, bf16[512,768]{1,0:T(8,128)(2,1)}, u32[]{:S(2)}, u32[]{:S(2)}) collective-permute-start(bf16[512,768]{1,0:T(8,128)(2,1)} %fusion.30), channel_id=1, source_target_pairs={{0,2},{1,3},{2,0},{3,1},{4,6},{5,7},{6,4},{7,5},{8,10},{9,11},{10,... | collective-permute-start | bytes 2359304 | tf_op jit(solution)/shard_map/ppermute | solution.py:873
  (59 other events, 182.2 us)
